TPU v7x, 32 devices: a whole 2x2x4 slice. The times are simulated.
32 devices in a mesh: row: 4 (over x, core), col: 8 (over z, y).
Axes of the slice: x: 2, y: 2, z: 4, core: 2. Of those that a mesh axis runs over, the one named last changes fastest.
Arguments:
- panel: bfloat16 [3072, 98304], P('row', 'col'), may hold values from -0.01953125 to 0.01953125
- surface: bfloat16 [98304, 1024], P('col'), may hold values from -6 to 6
- flexibility: float32 [4, 768, 768], P('row'), may hold values from -0.21875 to 0.21875
- owner_map: int32 [24], replicated, may hold values from 0 to 23, each once
- adjacency: int32 [4, 2], P('row'), may hold values from 0 to 3, as said below
- live_rows: int32 [24], replicated, may hold values from 1 to 128, 2304 in all
Outputs:
- response: float32 [1024, 98304], P('row', 'col')
Inputs may be any that keep to these rules, and one draw needn't show every extreme that they name: `adjacency`: each substructure lists 2 different neighbours, never itself. `owner_map`: every slot receives exactly one mortar block. `live_rows`: the live rows add up to 2304 and some block is full.
All inputs are finite; a program needn't handle non-finite values.
Results may differ from a plain program's by a relative error of at most 0.0029.
Values may be sent and summed in bfloat16 or wider, within the bound.
A program may use at most 192 MiB of HBM per device.

v0:
```python
import math

import jax
import jax.numpy as jnp
from jax import lax
from jax.sharding import PartitionSpec as P

MBLK = 128
ITERS = 2


DAMPING = 0.6
COUPLING = 0.5


def live_pattern(live_rows):
    offsets = jnp.arange(MBLK, dtype=jnp.int32)
    return (offsets[None, :] < live_rows[:, None]).astype(jnp.float32)


def body(panel, surface, flexibility, owner_map, adjacency, live_rows):
    order_rows, column_count = panel.shape
    row_total = lax.axis_size("row")
    col_total = lax.axis_size("col")
    own_row = lax.axis_index("row")
    load_total = surface.shape[1]
    load_share = load_total // col_total
    block_count = order_rows // MBLK
    traction = lax.psum_scatter(
        lax.dot_general(
            surface, panel, (((0,), (1,)), ((), ())), preferred_element_type=jnp.float32
        ),
        "col",
        scatter_dimension=0,
        tiled=True,
    )
    pattern = live_pattern(live_rows)
    own_pattern = lax.dynamic_slice_in_dim(pattern, own_row * block_count, block_count, 0)
    blocks = traction.reshape(load_share, block_count, MBLK) * own_pattern[None]
    every_block = lax.all_gather(blocks, "row", axis=1, tiled=True)
    block_total = owner_map.shape[0]
    inverse = (
        jnp.zeros((block_total,), jnp.int32)
        .at[owner_map]
        .set(jnp.arange(block_total, dtype=jnp.int32))
    )
    own_sources = lax.dynamic_slice_in_dim(inverse, own_row * block_count, block_count, 0)
    load_blocks = jnp.take(every_block, own_sources, axis=1).reshape(load_share, order_rows)
    hits = adjacency[0][:, None] == jnp.arange(row_total, dtype=jnp.int32)[None, :]
    neighbour_weights = jnp.sum(hits.astype(jnp.float32), axis=0)
    flex_local = flexibility[0]
    traces = jnp.zeros_like(load_blocks)
    for sweep_index in range(ITERS):
        coupled = load_blocks
        if sweep_index > 0:
            neighbours = lax.all_gather(traces[None], "row", axis=0, tiled=True)
            coupled = load_blocks + COUPLING * jnp.einsum(
                "n,nlo->lo", neighbour_weights, neighbours, precision=lax.Precision.HIGHEST
            )
        applied = lax.dot_general(
            coupled,
            flex_local,
            (((1,), (1,)), ((), ())),
            precision=lax.Precision.HIGHEST,
            preferred_element_type=jnp.float32,
        )
        traces = (1.0 - DAMPING) * traces + DAMPING * applied
    rounded = traces.astype(jnp.bfloat16).reshape(load_share, block_count, MBLK)
    every_trace = lax.all_gather(rounded, "row", axis=1, tiled=True)
    own_slots = lax.dynamic_slice_in_dim(owner_map, own_row * block_count, block_count, 0)
    updated = (
        jnp.take(every_trace, own_slots, axis=1) * own_pattern[None].astype(jnp.bfloat16)
    ).reshape(load_share, order_rows)
    all_loads = lax.all_gather(updated, "col", axis=0, tiled=True)
    gain_factor = math.sqrt(column_count * col_total / (order_rows * row_total))
    return lax.psum_scatter(
        gain_factor * jnp.dot(all_loads, panel, preferred_element_type=jnp.float32),
        "row",
        scatter_dimension=0,
        tiled=True,
    )


def solution(mesh):
    in_specs = (P("row", "col"), P("col", None), P("row", None, None), P(), P("row", None), P())
    out_specs = P("row", "col")
    return jax.shard_map(body, mesh=mesh, in_specs=in_specs, out_specs=out_specs, check_vma=False)
```

profile of v0, /device:TPU:0, one launch (start us, length us, event | category | flops | bytes accessed | tf_op | source)
XLA Modules:
  0.0 604.5 jit_solution(13668140794669306131)
XLA Ops:
  6.5 0.0 copy-start
  6.5 26.5 %fusion.25 = f32[1024,768]{1,0:T(8,128)} fusion(bf16[12288,1024]{1,0:T(8,128)(2,1)} %param.7, bf16[768,12288]{1,0:T(8,128)(2,1)} %param.6), kind=kOutput, calls=%fused_computation.40 | convolution fusion | flops 19327352832 | bytes 47185920 | tf_op jit(solution)/shard_map/dot_general | solution.py:30
  33.0 0.0 reduce-scatter.3.cloned.1.call-update
  33.1 0.0 all-gather.5.cloned.1.call-start
  33.1 0.6 copy-done.3
  33.7 0.1 dynamic-slice
  33.8 0.1 convert_bitcast_fusion
  33.8 76.6 %reduce-scatter.3.cloned.1.call-done = f32[128,768]{1,0:T(8,128)} async-done(((f32[1024,768]{1,0:T(8,128)}), f32[128,768]{1,0:T(8,128)}) %reduce-scatter.3.cloned.1.call-update) | async-done | bytes 393232 | tf_op jit(solution)/shard_map/reduce_scatter | solution.py:29
  110.4 1.1 copy.21
  111.6 0.2 broadcast_multiply_fusion.1
  111.7 0.9 copy.22
  112.7 0.0 all-gather.5.cloned.1.call-update
  112.7 0.0 all-gather.9.cloned.1.call-start
  112.8 0.6 scatter_custom_fusion
  113.4 0.1 compare_and_fusion
  113.5 0.0 copy-start.4
  113.5 18.0 %all-gather.5.cloned.1.call-done = f32[128,24,128]{2,0,1:T(8,128)} async-done(((f32[128,6,128]{2,0,1:T(8,128)}), f32[128,24,128]{2,0,1:T(8,128)}) %all-gather.5.cloned.1.call-update) | async-done | bytes 1572880 | tf_op jit(solution)/shard_map/all_gather | solution.py:40
  131.6 2.0 gather_fusion
  133.6 0.1 broadcast_select_fusion
  133.7 0.2 copy.23
  133.8 2.8 broadcast_multiply_fusion
  136.7 0.0 all-gather.9.cloned.1.call-update
  136.7 0.2 all-gather.7.cloned.1.call-start
  136.9 0.1 compare_and_fusion.1
  137.0 0.0 copy-done.4
  137.0 0.7 fusion.20
  137.7 0.1 broadcast_bitcast_fusion
  137.8 0.1 broadcast_bitcast_fusion.1
  137.9 0.2 copy.24
  138.0 0.2 bitcast_select_fusion
  138.2 18.3 %all-gather.9.cloned.1.call-done = f32[512,768]{1,0:T(8,128)} async-done(((f32[128,768]{1,0:T(8,128)}), f32[512,768]{1,0:T(8,128)}) %all-gather.9.cloned.1.call-update) | async-done | bytes 1572880 | tf_op jit(solution)/shard_map/all_gather | solution.py:56
  156.5 5.7 fusion.4
  162.2 1.2 copy.29
  163.4 3.2 fusion.12
  166.6 1.1 copy.25
  167.7 0.2 copy.26
  167.9 8.6 %all_gather.14 = bf16[128,24,128]{2,0,1:T(8,128)(2,1)S(1)} all-gather(bf16[128,6,128]{2,0,1:T(8,128)(2,1)S(1)} %copy.26), channel_id=1, replica_groups=mesh['row'=4,'col'=8] {'row'}, dimensions={1}, use_global_device_ids=true | all-gather | bytes 983040 | tf_op jit(solution)/shard_map/all_gather | solution.py:69
  176.5 0.6 gather_fusion.1
  177.1 0.2 copy.27
  177.3 1.0 fusion.17
  178.2 0.0 all-gather.7.cloned.1.call-update
  178.2 0.3 reduce-scatter.5.cloned.1.call-start
  178.5 44.3 %all-gather.7.cloned.1.call-done = bf16[1024,768]{0,1:T(8,128)(2,1)} async-done(((bf16[128,768]{0,1:T(8,128)(2,1)}), bf16[1024,768]{0,1:T(8,128)(2,1)}) %all-gather.7.cloned.1.call-update) | async-done | bytes 1572880 | tf_op jit(solution)/shard_map/all_gather | solution.py:74
  222.8 30.3 %convolution_multiply_fusion = f32[1024,12288]{1,0:T(8,128)} fusion(bf16[1024,768]{0,1:T(8,128)(2,1)} %all-gather.7.cloned.1.call-done, bf16[768,12288]{1,0:T(8,128)(2,1)} %param.6), kind=kOutput, calls=%fused_computation.3 | convolution fusion | flops 19339935744 | bytes 70778880 | tf_op jit(solution)/shard_map/dot_general | solution.py:77
  253.1 0.0 reduce-scatter.5.cloned.1.call-update
  253.1 0.0 copy-start.1
  253.1 344.8 %reduce-scatter.5.cloned.1.call-done = f32[256,12288]{1,0:T(8,128)} async-done(((f32[1024,12288]{1,0:T(8,128)}), f32[256,12288]{1,0:T(8,128)}) %reduce-scatter.5.cloned.1.call-update) | async-done | bytes 12582928 | tf_op jit(solution)/shard_map/reduce_scatter | solution.py:76
  597.9 0.0 copy-done.1
  (9 shorter events, 0.0 us)
Async XLA Ops:
  6.5 127.3 %copy-start = (f32[1,768,768]{2,1,0:T(8,128)S(1)}, f32[1,768,768]{2,1,0:T(8,128)}, u32[]{:S(2)}) copy-start(f32[1,768,768]{2,1,0:T(8,128)} %param.8) | copy-start | bytes 7077892
  6.5 103.9 %reduce-scatter.3.cloned.1.call-start = ((), (), s32[]{:S(2)}) async-start(), calls=%async_computation.2 | async-start | bytes 3538944 | tf_op jit(solution)/shard_map/reduce_scatter | solution.py:29
  33.0 0.7 copy-start.3
  33.0 79.7 %copy-start.2 = (s32[24]{0:T(128)S(1)}, s32[24]{0:T(128)}, u32[]{:S(2)}) copy-start(s32[24]{0:T(128)} %param.9) | copy-start | bytes 292
  33.1 98.5 %all-gather.5.cloned.1.call-start = ((), (), s32[]{:S(2)}) async-start(), calls=%async_computation.3 | async-start | bytes 1966080 | tf_op jit(solution)/shard_map/all_gather | solution.py:40
  112.7 43.8 %all-gather.9.cloned.1.call-start = ((), (), s32[]{:S(2)}) async-start(), calls=%async_computation.6 | async-start | bytes 1966080 | tf_op jit(solution)/shard_map/all_gather | solution.py:56
  113.5 23.5 %copy-start.4 = (s32[1,2]{1,0:T(1,128)S(1)}, s32[1,2]{1,0:T(1,128)}, u32[]{:S(2)}) copy-start(s32[1,2]{1,0:T(1,128)} %param.10) | copy-start | bytes 28
  136.7 86.1 %all-gather.7.cloned.1.call-start = ((), (), s32[]{:S(2)}) async-start(), calls=%async_computation.4 | async-start | bytes 1769472 | tf_op jit(solution)/shard_map/all_gather | solution.py:74
  178.2 419.7 %reduce-scatter.5.cloned.1.call-start = ((), (), s32[]{:S(2)}) async-start(), calls=%async_computation.5 | async-start | bytes 62914560 | tf_op jit(solution)/shard_map/reduce_scatter | solution.py:76
  253.1 344.9 %copy-start.1 = (f32[1,768,768]{2,1,0:T(8,128)S(1)}, f32[1,768,768]{2,1,0:T(8,128)}, u32[]{:S(2)}) copy-start(f32[1,768,768]{2,1,0:T(8,128)} %param.8) | copy-start | bytes 7077892
Sparse Core Ops, SparseCore 0:
  33.2 77.1 reduce-scatter.2
  112.8 18.7 all-gather.4
  136.8 19.6 all-gather.8
  178.4 44.4 all-gather.6
  253.2 344.6 reduce-scatter.4
where the time goes:
time: 605 us; the launch traced here: 604 us
  waiting for transfers between devices  502 us (83%)
  matrix products  68.5 us (11%)
  between operations  13.3 us (2%)
  local copies, waits for them, and re-layouts  9.05 us (1%)
  blocking collectives  8.58 us (1%)
    reduce_scatter x1, waiting for transfers between devices, body(): lax.psum_scatter(gain_factor * jnp.dot(all_loads, panel, preferred_elemen...  345 us
    reduce_scatter x1, waiting for transfers between devices, body(): lax.psum_scatter(lax.dot_general(surface, panel, (((0,), (1,)), ((), ()))...  76.6 us
    all_gather x1, waiting for transfers between devices, body(): all_loads = lax.all_gather(updated, 'col', axis=0, tiled=True)  44.3 us
    dot_general x1, matrix products, body(): jnp.dot(all_loads, panel, preferred_element_type=jnp.float32)  30.3 us
    dot_general x1, matrix products, body(): lax.dot_general(surface, panel, (((0,), (1,)), ((), ())), preferred_eleme...  26.5 us
    all_gather x1, waiting for transfers between devices, body(): neighbours = lax.all_gather(traces[None], 'row', axis=0, tiled=True)  18.3 us
    all_gather x1, waiting for transfers between devices, body(): every_block = lax.all_gather(blocks, 'row', axis=1, tiled=True)  18 us
  transfers between devices with their start and end apart: 5, of which 5 were waited for; matrix products, arithmetic and copies ran while one was open for 0% of the time, Pallas kernels for 0%

commit v1 on v0

--- a/solution.py
+++ b/solution.py
@@ -1,21 +1,75 @@
+import functools
 import math
 
 import jax
 import jax.numpy as jnp
 from jax import lax
+from jax.experimental import pallas as pl
+from jax.experimental.pallas import tpu as pltpu
 from jax.sharding import PartitionSpec as P
 
 MBLK = 128
 ITERS = 2
-
-
 DAMPING = 0.6
 COUPLING = 0.5
+TILE = 512
+GATHERED_SIXTEENTHS = 8
+PIECES = 3
 
 
 def live_pattern(live_rows):
     offsets = jnp.arange(MBLK, dtype=jnp.int32)
     return (offsets[None, :] < live_rows[:, None]).astype(jnp.float32)
+
+
+def product_kernel(count, gain, with_extra, with_base, *refs):
+    factors, panels = refs[:count], refs[count : 2 * count]
+    rest = refs[2 * count :]
+    total = jnp.dot(factors[0][...], panels[0][...], preferred_element_type=jnp.float32)
+    for factor, panel in zip(factors[1:], panels[1:]):
+        total += jnp.dot(factor[...], panel[...], preferred_element_type=jnp.float32)
+    total = gain * total
+    if with_extra:
+        total += rest[0][...].astype(jnp.float32)
+    rest[-1][...] = total.astype(rest[-1].dtype)
+
+
+def product(factors, panels, gain, columns, out_shape, out_start=0, extra=None, base=None):
+    starts, width = columns
+    count = len(factors)
+    rows, depth = factors[0].shape
+    in_specs = [pl.BlockSpec(f.shape, lambda j: (0, 0)) for f in factors]
+    for start in starts:
+        in_specs.append(
+            pl.BlockSpec((depth, TILE), functools.partial(lambda s, j: (0, s + j), start // TILE))
+        )
+    operands = list(factors) + list(panels)
+    if extra is not None:
+        in_specs.append(pl.BlockSpec((rows, TILE), lambda j: (0, j)))
+        operands.append(extra)
+    aliases = {}
+    if base is not None:
+        in_specs.append(pl.BlockSpec(memory_space=pl.ANY))
+        aliases = {len(operands): 0}
+        operands.append(base)
+    return pl.pallas_call(
+        functools.partial(product_kernel, count, gain, extra is not None, base is not None),
+        grid=(width // TILE,),
+        in_specs=in_specs,
+        out_specs=pl.BlockSpec(
+            (rows, TILE), functools.partial(lambda s, j: (0, s + j), out_start // TILE)
+        ),
+        out_shape=out_shape,
+        input_output_aliases=aliases,
+        compiler_params=pltpu.CompilerParams(
+            dimension_semantics=("arbitrary",), vmem_limit_bytes=40 * 1024 * 1024
+        ),
+        cost_estimate=pl.CostEstimate(
+            flops=2 * rows * depth * count * width,
+            bytes_accessed=2 * depth * count * width + 4 * rows * width,
+            transcendentals=0,
+        ),
+    )(*operands)
 
 
 def body(panel, surface, flexibility, owner_map, adjacency, live_rows):
@@ -25,14 +79,21 @@
     own_row = lax.axis_index("row")
     load_total = surface.shape[1]
     load_share = load_total // col_total
+    group = load_total // row_total
     block_count = order_rows // MBLK
+    swap = [(i, i ^ 1) for i in range(row_total)]
+    across = [(i, i ^ 2) for i in range(row_total)]
+
+    gathered = max(TILE, column_count * GATHERED_SIXTEENTHS // 16 // TILE * TILE)
+    far = lax.ppermute(panel[:, :gathered], "row", across)
+    partner = lax.ppermute(panel, "row", swap)
+    far_partner = lax.ppermute(far, "row", swap)
+
+    partial = lax.dot_general(
+        surface, panel, (((0,), (1,)), ((), ())), preferred_element_type=jnp.float32
+    )
     traction = lax.psum_scatter(
-        lax.dot_general(
-            surface, panel, (((0,), (1,)), ((), ())), preferred_element_type=jnp.float32
-        ),
-        "col",
-        scatter_dimension=0,
-        tiled=True,
+        partial.reshape(row_total, group, order_rows), "col", scatter_dimension=1, tiled=True
     )
     pattern = live_pattern(live_rows)
     own_pattern = lax.dynamic_slice_in_dim(pattern, own_row * block_count, block_count, 0)
@@ -65,20 +126,46 @@
             preferred_element_type=jnp.float32,
         )
         traces = (1.0 - DAMPING) * traces + DAMPING * applied
-    rounded = traces.astype(jnp.bfloat16).reshape(load_share, block_count, MBLK)
-    every_trace = lax.all_gather(rounded, "row", axis=1, tiled=True)
-    own_slots = lax.dynamic_slice_in_dim(owner_map, own_row * block_count, block_count, 0)
+    small = load_share // row_total
+    rounded = traces.astype(jnp.bfloat16).reshape(row_total, small, order_rows)
+    every_trace = lax.all_to_all(rounded, "row", split_axis=0, concat_axis=0, tiled=True)
+    every_trace = every_trace.reshape(row_total, small, block_count, MBLK)
+    every_trace = every_trace.transpose(1, 0, 2, 3).reshape(small, block_total, MBLK)
     updated = (
-        jnp.take(every_trace, own_slots, axis=1) * own_pattern[None].astype(jnp.bfloat16)
-    ).reshape(load_share, order_rows)
+        jnp.take(every_trace, owner_map, axis=1) * pattern[None].astype(jnp.bfloat16)
+    ).reshape(small, block_total * MBLK)
     all_loads = lax.all_gather(updated, "col", axis=0, tiled=True)
-    gain_factor = math.sqrt(column_count * col_total / (order_rows * row_total))
-    return lax.psum_scatter(
-        gain_factor * jnp.dot(all_loads, panel, preferred_element_type=jnp.float32),
-        "row",
-        scatter_dimension=0,
-        tiled=True,
+
+    def rows_of(source, index):
+        return lax.dynamic_slice_in_dim(source, index * order_rows, order_rows, 1)
+
+    other_a = lax.ppermute(rows_of(all_loads, own_row ^ 2), "row", across)
+    other_b = lax.ppermute(rows_of(all_loads, own_row ^ 3), "row", across)
+    mine = [rows_of(all_loads, own_row ^ k) for k in range(row_total)]
+
+    gain = math.sqrt(column_count * col_total / (order_rows * row_total))
+    width = column_count - gathered
+    edges = [width * k // PIECES // TILE * TILE for k in range(PIECES)] + [width]
+    arrivals = []
+    for low, high in zip(edges[:-1], edges[1:]):
+        start = gathered + low
+        piece = product(
+            [other_a, other_b],
+            [panel, partner],
+            gain,
+            ([start, start], high - low),
+            jax.ShapeDtypeStruct((group, high - low), jnp.bfloat16),
+        )
+        arrivals.append((start, high - low, lax.ppermute(piece, "row", across)))
+    full = jax.ShapeDtypeStruct((group, column_count), jnp.float32)
+    response = product(
+        mine, [panel, partner, far, far_partner], gain, ([0] * 4, gathered), full
     )
+    for start, size, arrived in arrivals:
+        response = product(
+            mine[:2], [panel, partner], gain, ([start, start], size), full, start, arrived, response
+        )
+    return response
 
 
 def solution(mesh):

time: 605 us -> 428 us (0.71)
  waiting for transfers between devices: 502 us -> 291 us
  Pallas kernels: 0 us -> 52.2 us
  matrix products: 68.5 us -> 38.2 us
  starting transfers between devices: 0.57 us -> 12.4 us
  local copies, waits for them, and re-layouts: 9.05 us -> 18.3 us
  blocking collectives: 8.58 us -> 0 us
    reduce_scatter x2 -> x1, waiting for transfers between devices: 421 us -> 74.1 us  [body(): lax.psum_scatter(partial.reshape(row_total, group, order_rows), 'col', sc...]
    ppermute x0 -> x8, waiting for transfers between devices: none -> 148 us  [the longest x1 109 us: body(): far = lax.ppermute(panel[:, :gathered], 'row', across)]
    pallas_call x0 -> x7, Pallas kernels: none -> 52.2 us  [product(): pl.pallas_call(functools.partial(product_kernel, count, gain, extra is no...]
    dot_general x1 -> x0, matrix products: 30.3 us -> none  [body(): jnp.dot(all_loads, panel, preferred_element_type=jnp.float32)]
    all_gather x1, waiting for transfers between devices: 18 us -> 0.02 us  [body(): every_block = lax.all_gather(blocks, 'row', axis=1, tiled=True)]
    slice x0 -> x1, local copies, waits for them, and re-layouts: none -> 8.81 us  [body(): far = lax.ppermute(panel[:, :gathered], 'row', across)]
    ppermute x0 -> x8, starting transfers between devices: none -> 8.69 us  [the longest x3 3.69 us: body(): arrivals.append((start, high - low, lax.ppermute(piece, 'row', across)))]
    all_gather x1 -> x0, blocking collectives: 8.58 us -> none  [body(): every_trace = lax.all_gather(rounded, 'row', axis=1, tiled=True)]
  transfers between devices with their start and end apart: 5 -> 13, of which waited for: 5 -> 9; matrix products, arithmetic and copies ran while one was open for 0% -> 14% of each run, Pallas kernels for 0% -> 11%
where the time goes in v1:
time: 428 us
  waiting for transfers between devices  291 us (68%)
  Pallas kernels  52.2 us (12%)
  matrix products  38.2 us (9%)
  local copies, waits for them, and re-layouts  18.3 us (4%)
  between operations  13.4 us (3%)
  starting transfers between devices  12.4 us (3%)
    ppermute x1, waiting for transfers between devices, body(): far = lax.ppermute(panel[:, :gathered], 'row', across)  109 us
    reduce_scatter x1, waiting for transfers between devices, body(): lax.psum_scatter(partial.reshape(row_total, group, order_rows), 'col', sc...  74.1 us
    pallas_call x7, Pallas kernels, product(): pl.pallas_call(functools.partial(product_kernel, count, gain, extra is no...  52.2 us
    all_gather x1, waiting for transfers between devices, body(): all_loads = lax.all_gather(updated, 'col', axis=0, tiled=True)  44.3 us
    dot_general x1, matrix products, body(): lax.dot_general(surface, panel, (((0,), (1,)), ((), ())), preferred_eleme...  26.4 us
    ppermute x3, waiting for transfers between devices, body(): arrivals.append((start, high - low, lax.ppermute(piece, 'row', across)))  22.6 us
    all_gather x1, waiting for transfers between devices, body(): neighbours = lax.all_gather(traces[None], 'row', axis=0, tiled=True)  19.6 us
    ppermute x1, waiting for transfers between devices, body(): other_a = lax.ppermute(rows_of(all_loads, own_row ^ 2), 'row', across)  9.96 us
  transfers between devices with their start and end apart: 13, of which 9 were waited for; matrix products, arithmetic and copies ran while one was open for 14% of the time, Pallas kernels for 11%

profile of v1, /device:TPU:0, one launch (start us, length us, event | category | flops | bytes accessed | tf_op | source)
XLA Modules:
  0.0 427.7 jit_solution(4355985767115594982)
XLA Ops:
  6.5 0.5 collective-permute-start
  7.0 8.8 %slice.3 = bf16[768,6144]{1,0:T(8,128)(2,1)} slice(bf16[768,12288]{1,0:T(8,128)(2,1)} %refs_2_.11), slice={[0:768], [0:6144]} | slice | bytes 18874368 | tf_op jit(solution)/shard_map/slice | solution.py:88
  15.8 2.4 collective-permute-start.6
  18.3 26.4 %fusion.25 = f32[1024,768]{1,0:T(8,128)} fusion(bf16[12288,1024]{1,0:T(8,128)(2,1)} %param.7, bf16[768,12288]{1,0:T(8,128)(2,1)} %refs_2_.11), kind=kOutput, calls=%fused_computation.43 | convolution fusion | flops 19327352832 | bytes 47185920 | tf_op jit(solution)/shard_map/dot_general | solution.py:92
  44.8 0.6 copy-done.2
  45.5 74.1 %reduce-scatter.2.cloned.1.call-done = f32[4,32,768]{2,1,0:T(8,128)} async-done(((f32[4,256,768]{2,1,0:T(8,128)}), f32[4,32,768]{2,1,0:T(8,128)}) %reduce-scatter.2.cloned.1.call-update) | async-done | bytes 393232 | tf_op jit(solution)/shard_map/reduce_scatter | solution.py:95
  119.6 1.1 reshape.85
  120.7 0.8 copy.20
  121.6 108.9 %collective-permute-done.6.refs_6_ = bf16[768,6144]{1,0:T(8,128)(2,1)} collective-permute-done((bf16[768,6144]{1,0:T(8,128)(2,1)}, bf16[768,6144]{1,0:T(8,128)(2,1)}, u32[]{:S(2)}, u32[]{:S(2)}) %collective-permute-start.6) | collective-permute-done | bytes 9437216 | tf_op jit(solution)/shard_map/ppermute | solution.py:88
  230.6 0.8 scatter_custom_fusion
  231.4 0.1 compare_and_fusion
  231.5 2.0 gather_fusion
  233.5 0.1 broadcast_select_fusion
  233.6 0.2 copy.21
  233.8 2.8 broadcast_multiply_fusion.1
  236.7 0.1 fusion.20
  236.8 1.2 compare_and_fusion.1
  238.0 0.1 lt.62
  238.1 0.2 copy.22
  238.3 0.2 bitcast_select_fusion
  238.5 19.6 %all-gather.9.cloned.1.call-done = f32[512,768]{1,0:T(8,128)} async-done(((f32[128,768]{1,0:T(8,128)}), f32[512,768]{1,0:T(8,128)}) %all-gather.9.cloned.1.call-update) | async-done | bytes 1572880 | tf_op jit(solution)/shard_map/all_gather | solution.py:117
  258.1 5.7 %fusion.4 = f32[1,128,768]{2,0,1:T(1,128)} fusion(f32[4,128,768]{2,1,0:T(8,128)} %bitcast.55, f32[4]{0:T(128)S(1)} %fusion.20), kind=kOutput, calls=%fused_computation.7 | convolution fusion | flops 4718592 | bytes 1966096 | tf_op jit(solution)/shard_map/n,nlo->lo/dot_general | solution.py:118
  263.8 1.2 copy.26
  265.0 3.2 fusion.12
  268.2 3.4 all-to-all-start
  271.6 0.3 all-gather.7.cloned.1.call-start
  272.0 4.9 %all-to-all-done = bf16[4,32,768]{2,1,0:T(8,128)(2,1)S(1)} async-done(((bf16[4,32,768]{2,1,0:T(8,128)(2,1)}), bf16[4,32,768]{2,1,0:T(8,128)(2,1)S(1)}, u32[]{:S(2)}, u32[]{:S(2)}) %all-to-all-start) | async-done | bytes 196640 | tf_op jit(solution)/shard_map/all_to_all | solution.py:131
  276.9 0.2 reshape.87
  277.2 0.6 gather_fusion.1
  277.8 0.7 fusion.17
  278.5 44.3 %all-gather.7.cloned.1.call-done = bf16[256,3072]{1,0:T(8,128)(2,1)} async-done(((bf16[32,3072]{1,0:T(8,128)(2,1)}), bf16[256,3072]{1,0:T(8,128)(2,1)}) %all-gather.7.cloned.1.call-update) | async-done | bytes 1572880 | tf_op jit(solution)/shard_map/all_gather | solution.py:137
  322.9 1.5 constant_dynamic-slice_fusion.3
  324.3 1.5 collective-permute-start.1
  325.8 0.6 collective-permute-start.2
  326.4 10.0 %collective-permute-done.1.refs_0_ = bf16[256,768]{1,0:T(8,128)(2,1)S(1)} collective-permute-done((bf16[256,768]{1,0:T(8,128)(2,1)S(1)}, bf16[256,768]{1,0:T(8,128)(2,1)S(1)}, u32[]{:S(2)}, u32[]{:S(2)}) %collective-permute-start.1) | collective-permute-done | bytes 393248 | tf_op jit(solution)/shard_map/ppermute | solution.py:142
  336.4 6.3 %collective-permute-done.2.refs_1_ = bf16[256,768]{1,0:T(8,128)(2,1)S(1)} collective-permute-done((bf16[256,768]{1,0:T(8,128)(2,1)S(1)}, bf16[256,768]{1,0:T(8,128)(2,1)S(1)}, u32[]{:S(2)}, u32[]{:S(2)}) %collective-permute-start.2) | collective-permute-done | bytes 393248 | tf_op jit(solution)/shard_map/ppermute | solution.py:143
  342.6 4.7 %shard_map.66 = bf16[256,2048]{1,0:T(8,128)(2,1)S(1)} custom-call(bf16[256,768]{1,0:T(8,128)(2,1)S(1)} %collective-permute-done.1.refs_0_, bf16[256,768]{1,0:T(8,128)(2,1)S(1)} %collective-permute-done.2.refs_1_, bf16[768,12288]{1,0:T(8,128)(2,1)} %refs_2_.11, bf16[768,12288]{1,0:T(8,128)(2,1)} %collective-permute-done.refs_3_.refs_5_), custom_call_target="tpu_custom_call" | custom-call | flops 1610612736 | bytes 8388608 | tf_op jit(solution)/shard_map/pallas_call | solution.py:55
  347.3 1.5 collective-permute-start.5
  348.9 4.7 %shard_map.65 = bf16[256,2048]{1,0:T(8,128)(2,1)S(1)} custom-call(bf16[256,768]{1,0:T(8,128)(2,1)S(1)} %collective-permute-done.1.refs_0_, bf16[256,768]{1,0:T(8,128)(2,1)S(1)} %collective-permute-done.2.refs_1_, bf16[768,12288]{1,0:T(8,128)(2,1)} %refs_2_.11, bf16[768,12288]{1,0:T(8,128)(2,1)} %collective-permute-done.refs_3_.refs_5_), custom_call_target="tpu_custom_call" | custom-call | flops 1610612736 | bytes 8388608 | tf_op jit(solution)/shard_map/pallas_call | solution.py:55
  353.6 0.6 collective-permute-start.4
  354.2 4.7 %shard_map.64 = bf16[256,2048]{1,0:T(8,128)(2,1)S(1)} custom-call(bf16[256,768]{1,0:T(8,128)(2,1)S(1)} %collective-permute-done.1.refs_0_, bf16[256,768]{1,0:T(8,128)(2,1)S(1)} %collective-permute-done.2.refs_1_, bf16[768,12288]{1,0:T(8,128)(2,1)} %refs_2_.11, bf16[768,12288]{1,0:T(8,128)(2,1)} %collective-permute-done.refs_3_.refs_5_), custom_call_target="tpu_custom_call" | custom-call | flops 1610612736 | bytes 8388608 | tf_op jit(solution)/shard_map/pallas_call | solution.py:55
  358.9 1.5 collective-permute-start.3
  360.4 20.9 %shard_map.67.refs_5_ = f32[256,12288]{1,0:T(8,128)} custom-call(bf16[256,768]{1,0:T(8,128)(2,1)S(1)} %get-tuple-element.10.refs_0_, bf16[256,768]{1,0:T(8,128)(2,1)S(1)} %get-tuple-element.9.refs_1_, bf16[256,768]{1,0:T(8,128)(2,1)S(1)} %get-tuple-element.8.refs_2_, bf16[256,768]{1,0:T(8,128)(2,1)S(1)} %get-tuple-element.7.refs_3_, ...), custom_call_target="tpu_custom_call" | custom-call | flops 9663676416 | bytes 44040192 | tf_op jit(solution)/shard_map/pallas_call | solution.py:55
  381.3 5.7 %shard_map.68.refs_5_ = f32[256,12288]{1,0:T(8,128)} custom-call(bf16[256,768]{1,0:T(8,128)(2,1)S(1)} %get-tuple-element.10.refs_0_, bf16[256,768]{1,0:T(8,128)(2,1)S(1)} %get-tuple-element.9.refs_1_, bf16[768,12288]{1,0:T(8,128)(2,1)} %refs_2_.11, bf16[768,12288]{1,0:T(8,128)(2,1)} %collective-permute-done.refs_3_.refs_5_, ...), custom_call_target="tpu_custom_call", output_to_operand_aliasing={{}: (5, {})} | custom-call | flops 1610612736 | bytes 8388608 | tf_op jit(solution)/shard_map/pallas_call | solution.py:55
  387.0 8.9 %collective-permute-done.4.refs_4_ = bf16[256,2048]{1,0:T(8,128)(2,1)S(1)} collective-permute-done((bf16[256,2048]{1,0:T(8,128)(2,1)S(1)}, bf16[256,2048]{1,0:T(8,128)(2,1)S(1)}, u32[]{:S(2)}, u32[]{:S(2)}) %collective-permute-start.4) | collective-permute-done | bytes 1048608 | tf_op jit(solution)/shard_map/ppermute | solution.py:159
  395.9 5.7 %shard_map.69.refs_5_ = f32[256,12288]{1,0:T(8,128)} custom-call(bf16[256,768]{1,0:T(8,128)(2,1)S(1)} %get-tuple-element.10.refs_0_, bf16[256,768]{1,0:T(8,128)(2,1)S(1)} %get-tuple-element.9.refs_1_, bf16[768,12288]{1,0:T(8,128)(2,1)} %refs_2_.11, bf16[768,12288]{1,0:T(8,128)(2,1)} %collective-permute-done.refs_3_.refs_5_, ...), custom_call_target="tpu_custom_call", output_to_operand_aliasing={{}: (5, {})} | custom-call | flops 1610612736 | bytes 8388608 | tf_op jit(solution)/shard_map/pallas_call | solution.py:55
  401.6 13.8 %collective-permute-done.3.refs_4_ = bf16[256,2048]{1,0:T(8,128)(2,1)S(1)} collective-permute-done((bf16[256,2048]{1,0:T(8,128)(2,1)S(1)}, bf16[256,2048]{1,0:T(8,128)(2,1)S(1)}, u32[]{:S(2)}, u32[]{:S(2)}) %collective-permute-start.3) | collective-permute-done | bytes 1048608 | tf_op jit(solution)/shard_map/ppermute | solution.py:159
  415.4 5.8 %shard_map.70 = f32[256,12288]{1,0:T(8,128)} custom-call(bf16[256,768]{1,0:T(8,128)(2,1)S(1)} %get-tuple-element.10.refs_0_, bf16[256,768]{1,0:T(8,128)(2,1)S(1)} %get-tuple-element.9.refs_1_, bf16[768,12288]{1,0:T(8,128)(2,1)} %refs_2_.11, bf16[768,12288]{1,0:T(8,128)(2,1)} %collective-permute-done.refs_3_.refs_5_, ...), custom_call_target="tpu_custom_call", output_to_operand_aliasing={{}: (5, {})} | custom-call | flops 1610612736 | bytes 8388608 | tf_op jit(solution)/shard_map/pallas_call | solution.py:55
  (38 shorter events, 0.6 us)
Async XLA Ops:
  6.5 227.3 %copy-start = (f32[1,768,768]{2,1,0:T(8,128)S(1)}, f32[1,768,768]{2,1,0:T(8,128)}, u32[]{:S(2)}) copy-start(f32[1,768,768]{2,1,0:T(8,128)} %param.8) | copy-start | bytes 7077892
  6.5 113.0 %reduce-scatter.2.cloned.1.call-start = ((), (), s32[]{:S(2)}) async-start(), calls=%async_computation.2 | async-start | bytes 3538944 | tf_op jit(solution)/shard_map/reduce_scatter | solution.py:95
  6.5 336.1 %collective-permute-start = (bf16[768,12288]{1,0:T(8,128)(2,1)}, bf16[768,12288]{1,0:T(8,128)(2,1)}, u32[]{:S(2)}, u32[]{:S(2)}) collective-permute-start(bf16[768,12288]{1,0:T(8,128)(2,1)} %refs_2_.11), channel_id=1, source_target_pairs={{0,8},{8,0},{16,24},{24,16},{1,9},{9,1},{17,25},{25,17},{2,10},{10... | collective-permute-start | bytes 56623112 | tf_op jit(solution)/shard_map/ppermute | solution.py:89
  15.8 214.7 %collective-permute-start.6 = (bf16[768,6144]{1,0:T(8,128)(2,1)}, bf16[768,6144]{1,0:T(8,128)(2,1)}, u32[]{:S(2)}, u32[]{:S(2)}) collective-permute-start(bf16[768,6144]{1,0:T(8,128)(2,1)} %slice.3), channel_id=1, source_target_pairs={{0,16},{8,24},{16,0},{24,8},{1,17},{9,25},{17,1},{25,9},{2,18},{10... | collective-permute-start | bytes 28311560 | tf_op jit(solution)/shard_map/ppermute | solution.py:88
  44.7 0.7 copy-start.2
  44.7 185.9 %copy-start.7 = (s32[24]{0:T(128)S(1)}, s32[24]{0:T(128)}, u32[]{:S(2)}) copy-start(s32[24]{0:T(128)} %param.9) | copy-start | bytes 292
  44.7 186.8 %all-gather.5.cloned.1.call-start = ((), (), s32[]{:S(2)}) async-start(), calls=%async_computation.3 | async-start | bytes 1966080 | tf_op jit(solution)/shard_map/all_gather | solution.py:101
  121.5 136.6 %all-gather.9.cloned.1.call-start = ((), (), s32[]{:S(2)}) async-start(), calls=%async_computation.5 | async-start | bytes 1966080 | tf_op jit(solution)/shard_map/all_gather | solution.py:117
  230.5 129.9 %collective-permute-start.7 = (bf16[768,6144]{1,0:T(8,128)(2,1)}, bf16[768,6144]{1,0:T(8,128)(2,1)}, u32[]{:S(2)}, u32[]{:S(2)}) collective-permute-start(bf16[768,6144]{1,0:T(8,128)(2,1)} %collective-permute-done.6.refs_6_), channel_id=1, source_target_pairs={{0,8},{8,0},{16,24},{24,16},{1,9},{9,1},{17,25},{25,17},{2,10},{10... | collective-permute-start | bytes 28311560 | tf_op jit(solution)/shard_map/ppermute | solution.py:90
  230.5 0.9 copy-start.3
  231.5 5.2 %copy-start.6 = (s32[1,2]{1,0:T(1,128)S(1)}, s32[1,2]{1,0:T(1,128)}, u32[]{:S(2)}) copy-start(s32[1,2]{1,0:T(1,128)} %param.10) | copy-start | bytes 28
  258.1 13.9 %copy-start.4 = (s32[24]{0:T(128)S(1)}, s32[24]{0:T(128)}, u32[]{:S(2)}) copy-start(s32[24]{0:T(128)} %copy-done.3) | copy-start | bytes 292
  263.8 8.1 %copy-start.5 = (pred[24]{0:T(512)(128)(4,1)S(1)}, pred[24]{0:T(512)(128)(4,1)}, u32[]{:S(2)}) copy-start(pred[24]{0:T(512)(128)(4,1)} %compare_and_fusion.1) | copy-start | bytes 76
  268.2 8.6 %all-to-all-start = ((bf16[4,32,768]{2,1,0:T(8,128)(2,1)}), bf16[4,32,768]{2,1,0:T(8,128)(2,1)S(1)}, u32[]{:S(2)}, u32[]{:S(2)}) async-start(bf16[4,32,768]{2,1,0:T(8,128)(2,1)} %bitcast.57), calls=%async_computation.1 | async-start | bytes 393216 | tf_op jit(solution)/shard_map/all_to_all | solution.py:131
  271.6 51.2 %all-gather.7.cloned.1.call-start = ((), (), s32[]{:S(2)}) async-start(), calls=%async_computation.4 | async-start | bytes 1769472 | tf_op jit(solution)/shard_map/all_gather | solution.py:137
  324.3 12.1 %collective-permute-start.1 = (bf16[256,768]{1,0:T(8,128)(2,1)S(1)}, bf16[256,768]{1,0:T(8,128)(2,1)S(1)}, u32[]{:S(2)}, u32[]{:S(2)}) collective-permute-start(bf16[256,768]{1,0:T(8,128)(2,1)S(1)} %get-tuple-element.8.refs_2_), channel_id=1, source_target_pairs={{0,16},{8,24},{16,0},{24,8},{1,17},{9,25},{17,1},{25,9},{2,18},{10... | collective-permute-start | bytes 1179656 | tf_op jit(solution)/shard_map/ppermute | solution.py:142
  325.8 16.8 %collective-permute-start.2 = (bf16[256,768]{1,0:T(8,128)(2,1)S(1)}, bf16[256,768]{1,0:T(8,128)(2,1)S(1)}, u32[]{:S(2)}, u32[]{:S(2)}) collective-permute-start(bf16[256,768]{1,0:T(8,128)(2,1)S(1)} %get-tuple-element.7.refs_3_), channel_id=1, source_target_pairs={{0,16},{8,24},{16,0},{24,8},{1,17},{9,25},{17,1},{25,9},{2,18},{10... | collective-permute-start | bytes 1179656 | tf_op jit(solution)/shard_map/ppermute | solution.py:143
  347.3 34.0 %collective-permute-start.5 = (bf16[256,2048]{1,0:T(8,128)(2,1)S(1)}, bf16[256,2048]{1,0:T(8,128)(2,1)S(1)}, u32[]{:S(2)}, u32[]{:S(2)}) collective-permute-start(bf16[256,2048]{1,0:T(8,128)(2,1)S(1)} %shard_map.66), channel_id=1, source_target_pairs={{0,16},{8,24},{16,0},{24,8},{1,17},{9,25},{17,1},{25,9},{2,18},{10... | collective-permute-start | bytes 3145736 | tf_op jit(solution)/shard_map/ppermute | solution.py:159
  353.6 42.3 %collective-permute-start.4 = (bf16[256,2048]{1,0:T(8,128)(2,1)S(1)}, bf16[256,2048]{1,0:T(8,128)(2,1)S(1)}, u32[]{:S(2)}, u32[]{:S(2)}) collective-permute-start(bf16[256,2048]{1,0:T(8,128)(2,1)S(1)} %shard_map.65), channel_id=1, source_target_pairs={{0,16},{8,24},{16,0},{24,8},{1,17},{9,25},{17,1},{25,9},{2,18},{10... | collective-permute-start | bytes 3145736 | tf_op jit(solution)/shard_map/ppermute | solution.py:159
  358.9 56.5 %collective-permute-start.3 = (bf16[256,2048]{1,0:T(8,128)(2,1)S(1)}, bf16[256,2048]{1,0:T(8,128)(2,1)S(1)}, u32[]{:S(2)}, u32[]{:S(2)}) collective-permute-start(bf16[256,2048]{1,0:T(8,128)(2,1)S(1)} %shard_map.64), channel_id=1, source_target_pairs={{0,16},{8,24},{16,0},{24,8},{1,17},{9,25},{17,1},{25,9},{2,18},{10... | collective-permute-start | bytes 3145736 | tf_op jit(solution)/shard_map/ppermute | solution.py:159
  415.4 5.8 %copy-start.1 = (f32[1,768,768]{2,1,0:T(8,128)S(1)}, f32[1,768,768]{2,1,0:T(8,128)}, u32[]{:S(2)}) copy-start(f32[1,768,768]{2,1,0:T(8,128)} %param.8) | copy-start | bytes 7077892
Sparse Core Ops, SparseCore 0:
  44.8 74.7 reduce-scatter.1
  121.7 27.1 all-gather.4
  236.8 21.2 all-gather.8
  278.6 44.1 all-gather.6

commit v2 on v1

v2 whole, which is shorter than its diff:
```python
import functools
import math

import jax
import jax.numpy as jnp
from jax import lax
from jax.experimental import pallas as pl
from jax.experimental.pallas import tpu as pltpu
from jax.sharding import PartitionSpec as P

MBLK = 128
ITERS = 2
DAMPING = 0.6
COUPLING = 0.5
TILE = 512
GATHERED_SIXTEENTHS = 5
MESH = pl.DeviceIdType.MESH
PIECES = 3


def live_pattern(live_rows):
    offsets = jnp.arange(MBLK, dtype=jnp.int32)
    return (offsets[None, :] < live_rows[:, None]).astype(jnp.float32)


def product_kernel(count, gain, with_extra, with_base, *refs):
    factors, panels = refs[:count], refs[count : 2 * count]
    rest = refs[2 * count :]
    total = jnp.dot(factors[0][...], panels[0][...], preferred_element_type=jnp.float32)
    for factor, panel in zip(factors[1:], panels[1:]):
        total += jnp.dot(factor[...], panel[...], preferred_element_type=jnp.float32)
    total = gain * total
    if with_extra:
        total += rest[0][...].astype(jnp.float32)
    rest[-1][...] = total.astype(rest[-1].dtype)


def product(loads, depth, first, panels, gain, columns, out_shape, out_start=0, extra=None, base=None):
    starts, width = columns
    count = len(panels)
    rows = loads.shape[0]
    in_specs = [
        pl.BlockSpec((rows, depth), functools.partial(lambda k, j: (0, k), first + k))
        for k in range(count)
    ]
    for start in starts:
        in_specs.append(
            pl.BlockSpec((depth, TILE), functools.partial(lambda s, j: (0, s + j), start // TILE))
        )
    operands = [loads] * count + list(panels)
    if extra is not None:
        in_specs.append(pl.BlockSpec((rows, TILE), lambda j: (0, j)))
        operands.append(extra)
    aliases = {}
    if base is not None:
        in_specs.append(pl.BlockSpec(memory_space=pl.ANY))
        aliases = {len(operands): 0}
        operands.append(base)
    return pl.pallas_call(
        functools.partial(product_kernel, count, gain, extra is not None, base is not None),
        grid=(width // TILE,),
        in_specs=in_specs,
        out_specs=pl.BlockSpec(
            (rows, TILE), functools.partial(lambda s, j: (0, s + j), out_start // TILE)
        ),
        out_shape=out_shape,
        input_output_aliases=aliases,
        compiler_params=pltpu.CompilerParams(
            dimension_semantics=("arbitrary",), vmem_limit_bytes=40 * 1024 * 1024
        ),
        cost_estimate=pl.CostEstimate(
            flops=2 * rows * depth * count * width,
            bytes_accessed=2 * depth * count * width + 4 * rows * width,
            transcendentals=0,
        ),
    )(*operands)


def greet(axis, peers):
    barrier = pltpu.get_barrier_semaphore()
    for peer in peers:
        pl.semaphore_signal(barrier, inc=1, device_id={axis: peer}, device_id_type=MESH)
    pl.semaphore_wait(barrier, len(peers))


def send(axis, peer, source, target, send_sem, recv_sem):
    copy = pltpu.make_async_remote_copy(
        src_ref=source,
        dst_ref=target,
        send_sem=send_sem,
        recv_sem=recv_sem,
        device_id={axis: peer},
        device_id_type=MESH,
    )
    copy.start()
    return copy


def gather_kernel(axis, n, in_ref, out_ref, far_send, far_recv, near_send, near_recv):
    me = lax.axis_index(axis)
    inner, place, outer = me % 2, me // 2, n // 2
    partner = me + 1 - 2 * inner
    peers = [((place + k) % outer) * 2 + inner for k in range(1, outer)]
    greet(axis, [partner] + peers)
    far = []
    for k in range(1, outer):
        far.append(
            send(axis, peers[k - 1], in_ref, out_ref.at[me], far_send.at[k], far_recv.at[k])
        )
    near = [send(axis, partner, in_ref, out_ref.at[me], near_send.at[0], near_recv.at[0])]
    out_ref[me] = in_ref[...]
    for k in range(1, outer):
        source = ((place - k + outer) % outer) * 2 + inner
        far[k - 1].wait_recv()
        slot = out_ref.at[source]
        near.append(send(axis, partner, slot, slot, near_send.at[k], near_recv.at[k]))
    for copy in far:
        copy.wait_send()
    for copy in near:
        copy.wait()


def gather(block, axis, n, ident):
    return pl.pallas_call(
        functools.partial(gather_kernel, axis, n),
        out_shape=jax.ShapeDtypeStruct((n,) + block.shape, block.dtype),
        in_specs=[pl.BlockSpec(memory_space=pltpu.VMEM)],
        out_specs=pl.BlockSpec(memory_space=pltpu.VMEM),
        scratch_shapes=[pltpu.SemaphoreType.DMA((n // 2,))] * 4,
        compiler_params=pltpu.CompilerParams(collective_id=ident, has_side_effects=True),
    )(block)


def reduce_kernel(axis, n, part, out_ref, near_in, held, far_in, near_send, near_recv, far_send, far_recv):
    me = lax.axis_index(axis)
    inner, place, outer = me % 2, me // 2, n // 2
    partner = me + 1 - 2 * inner
    peers = [((place + k) % outer) * 2 + inner for k in range(outer)]
    greet(axis, [partner] + peers[1:])
    order = list(range(1, outer)) + [0]
    near = {}
    for k in order:
        near[k] = send(
            axis,
            partner,
            part.at[:, peers[k] + 1 - 2 * inner],
            near_in.at[k],
            near_send.at[k],
            near_recv.at[k],
        )
    far = {}
    for k in order[:-1]:
        near[k].wait_recv()
        held[k] = part[:, peers[k]] + near_in[k]
        far[k] = send(axis, peers[k], held.at[k], far_in.at[k], far_send.at[k], far_recv.at[k])
    near[0].wait_recv()
    out_ref[...] = part[:, me] + near_in[0]
    for k in order[:-1]:
        far[k].wait_recv()
        out_ref[...] += far_in[k]
    for k in order[:-1]:
        far[k].wait_send()
    for k in order:
        near[k].wait_send()


def reduce_scatter(partial, axis, n, ident):
    groups, _, rows, width = partial.shape
    block = (groups, rows, width)
    slots = pltpu.VMEM((n // 2,) + block, jnp.float32)
    return pl.pallas_call(
        functools.partial(reduce_kernel, axis, n),
        out_shape=jax.ShapeDtypeStruct(block, jnp.float32),
        in_specs=[pl.BlockSpec(memory_space=pltpu.VMEM)],
        out_specs=pl.BlockSpec(memory_space=pltpu.VMEM),
        scratch_shapes=[slots] * 3 + [pltpu.SemaphoreType.DMA((n // 2,))] * 4,
        compiler_params=pltpu.CompilerParams(collective_id=ident, has_side_effects=True),
    )(partial)


def swap_kernel(axis, in_ref, token_ref, out_ref, send_sem, recv_sem):
    del token_ref
    me = lax.axis_index(axis)
    partner = me + 1 - 2 * (me % 2)
    greet(axis, [partner])
    send(axis, partner, in_ref, out_ref, send_sem, recv_sem).wait()


def swap_after(array, token, axis, ident):
    return pl.pallas_call(
        functools.partial(swap_kernel, axis),
        out_shape=jax.ShapeDtypeStruct(array.shape, array.dtype),
        in_specs=[pl.BlockSpec(memory_space=pl.ANY)] * 2,
        out_specs=pl.BlockSpec(memory_space=pl.ANY),
        scratch_shapes=[pltpu.SemaphoreType.DMA] * 2,
        compiler_params=pltpu.CompilerParams(collective_id=ident, has_side_effects=True),
    )(array, token)


def body(panel, surface, flexibility, owner_map, adjacency, live_rows):
    order_rows, column_count = panel.shape
    row_total = lax.axis_size("row")
    col_total = lax.axis_size("col")
    own_row = lax.axis_index("row")
    load_total = surface.shape[1]
    load_share = load_total // col_total
    group = load_total // row_total
    small = group // col_total
    block_count = order_rows // MBLK
    block_total = owner_map.shape[0]
    swap = [(i, i ^ 1) for i in range(row_total)]
    across = [(i, i ^ 2) for i in range(row_total)]

    gathered = max(TILE, column_count * GATHERED_SIXTEENTHS // 16 // TILE * TILE)
    far = lax.ppermute(panel[:, :gathered], "row", across)
    partner = lax.ppermute(panel, "row", swap)

    partial = lax.dot_general(
        surface, panel, (((0,), (1,)), ((), ())), preferred_element_type=jnp.float32
    )
    traction = reduce_scatter(
        partial.reshape(row_total, col_total, small, order_rows), "col", col_total, 0
    ).reshape(load_share, order_rows)
    pattern = live_pattern(live_rows)
    own_pattern = lax.dynamic_slice_in_dim(pattern, own_row * block_count, block_count, 0)
    masked = traction * own_pattern.reshape(1, order_rows)
    every_block = gather(masked, "row", row_total, 1)
    every_block = every_block.reshape(row_total, load_share, block_count, MBLK)
    inverse = (
        jnp.zeros((block_total,), jnp.int32)
        .at[owner_map]
        .set(jnp.arange(block_total, dtype=jnp.int32))
    )
    own_sources = lax.dynamic_slice_in_dim(inverse, own_row * block_count, block_count, 0)
    every_block = every_block.transpose(0, 2, 1, 3).reshape(block_total, load_share, MBLK)
    load_blocks = jnp.take(every_block, own_sources, axis=0)
    load_blocks = load_blocks.transpose(1, 0, 2).reshape(load_share, order_rows)
    hits = adjacency[0][:, None] == jnp.arange(row_total, dtype=jnp.int32)[None, :]
    neighbour_weights = jnp.sum(hits.astype(jnp.float32), axis=0)
    flex_local = flexibility[0]
    traces = jnp.zeros_like(load_blocks)
    for sweep_index in range(ITERS):
        coupled = load_blocks
        if sweep_index > 0:
            neighbours = gather(traces, "row", row_total, 1 + sweep_index)
            coupled = load_blocks + COUPLING * jnp.sum(
                neighbour_weights[:, None, None] * neighbours, axis=0
            )
        applied = lax.dot_general(
            coupled,
            flex_local,
            (((1,), (1,)), ((), ())),
            precision=lax.Precision.HIGHEST,
            preferred_element_type=jnp.float32,
        )
        traces = (1.0 - DAMPING) * traces + DAMPING * applied
    every_trace = gather(traces.astype(jnp.bfloat16), "row", row_total, 1 + ITERS)
    every_trace = every_trace.reshape(row_total, row_total, small, block_count, MBLK)
    blocks = jnp.concatenate(
        [(own_row ^ k) * block_count + jnp.arange(block_count) for k in range(row_total)]
    )
    slots = jnp.take(owner_map, blocks)
    masks = jnp.take(pattern, blocks, axis=0).astype(jnp.bfloat16)

    def updated_for(load_group, count):
        mine = lax.dynamic_index_in_dim(every_trace, load_group, 1, keepdims=False)
        mine = mine.transpose(0, 2, 1, 3).reshape(block_total, small, MBLK)
        mine = jnp.take(mine, slots[:count], axis=0) * masks[:count, None, :]
        return mine.transpose(1, 0, 2).reshape(small, count * MBLK)

    wanted = jnp.concatenate(
        [updated_for(own_row, block_total), updated_for(own_row ^ 2, 2 * block_count)], axis=1
    )
    all_loads = gather(wanted, "col", col_total, 2 + ITERS).reshape(group, -1)

    gain = math.sqrt(column_count * col_total / (order_rows * row_total))
    width = column_count - gathered
    edges = [width * k // PIECES // TILE * TILE for k in range(PIECES)] + [width]
    arrivals = []
    for low, high in zip(edges[:-1], edges[1:]):
        start = gathered + low
        piece = product(
            all_loads,
            order_rows,
            row_total,
            [panel, partner],
            gain,
            ([start, start], high - low),
            jax.ShapeDtypeStruct((group, high - low), jnp.bfloat16),
        )
        arrivals.append((start, high - low, lax.ppermute(piece, "row", across)))
    far_partner = swap_after(far, piece, "row", 3 + ITERS)
    full = jax.ShapeDtypeStruct((group, column_count), jnp.float32)
    response = product(
        all_loads,
        order_rows,
        0,
        [panel, partner, far, far_partner],
        gain,
        ([0] * row_total, gathered),
        full,
    )
    for start, size, arrived in arrivals:
        response = product(
            all_loads,
            order_rows,
            0,
            [panel, partner],
            gain,
            ([start, start], size),
            full,
            start,
            arrived,
            response,
        )
    return response


def solution(mesh):
    in_specs = (P("row", "col"), P("col", None), P("row", None, None), P(), P("row", None), P())
    out_specs = P("row", "col")
    return jax.shard_map(body, mesh=mesh, in_specs=in_specs, out_specs=out_specs, check_vma=False)
```

time: 428 us -> 353 us (0.82)
  waiting for transfers between devices: 291 us -> 39.2 us
  Pallas kernels: 52.2 us -> 237 us
  between operations: 13.4 us -> 0.3 us
  local copies, waits for them, and re-layouts: 18.3 us -> 27.3 us
  starting transfers between devices: 12.4 us -> 6.42 us
  matrix products: 38.2 us -> 32.5 us
    pallas_call x0 -> x6, Pallas kernels: none -> 179 us  [the longest x4 118 us: gather(): pl.pallas_call(functools.partial(gather_kernel, axis, n), out_shape=jax.S...]
    ppermute x1, waiting for transfers between devices: 109 us -> 0.01 us  [body(): far = lax.ppermute(panel[:, :gathered], 'row', across)]
    reduce_scatter x1 -> x0, waiting for transfers between devices: 74.1 us -> none  [body(): lax.psum_scatter(partial.reshape(row_total, group, order_rows), 'col', sc...]
    all_gather x3 -> x0, waiting for transfers between devices: 63.9 us -> none  [the longest x1 44.3 us: body(): all_loads = lax.all_gather(updated, 'col', axis=0, tiled=True)]
    ppermute x3, waiting for transfers between devices: 22.6 us -> 39.2 us  [body(): arrivals.append((start, high - low, lax.ppermute(piece, 'row', across)))]
    ppermute x3 -> x0, waiting for transfers between devices: 16.2 us -> none  [the longest x1 9.96 us: body(): other_a = lax.ppermute(rows_of(all_loads, own_row ^ 2), 'row', across)]
    pallas_call x7, Pallas kernels: 52.2 us -> 58.5 us  [product(): pl.pallas_call(functools.partial(product_kernel, count, gain, extra is no...]
    dot_general x1 -> x0, matrix products: 5.68 us -> none  [body(): jnp.einsum('n,nlo->lo', neighbour_weights, neighbours, precision=lax.Prec...]
  transfers between devices with their start and end apart: 13 -> 5, of which waited for: 9 -> 2; matrix products, arithmetic and copies ran while one was open for 14% -> 18% of each run, Pallas kernels for 11% -> 65%
where the time goes in v2:
time: 353 us; the launch traced here: 349 us
  Pallas kernels  237 us (67%)
  waiting for transfers between devices  39.2 us (11%)
  matrix products  32.5 us (9%)
  local copies, waits for them, and re-layouts  27.3 us (8%)
  other arithmetic  6.51 us (2%)
  starting transfers between devices  6.42 us (2%)
    pallas_call x4, Pallas kernels, gather(): pl.pallas_call(functools.partial(gather_kernel, axis, n), out_shape=jax.S...  118 us
    pallas_call x7, Pallas kernels, product(): pl.pallas_call(functools.partial(product_kernel, count, gain, extra is no...  58.5 us
    pallas_call x1, Pallas kernels, reduce_scatter(): pl.pallas_call(functools.partial(reduce_kernel, axis, n), out_shape=jax.S...  51.5 us
    ppermute x3, waiting for transfers between devices, body(): arrivals.append((start, high - low, lax.ppermute(piece, 'row', across)))  39.2 us
    dot_general x1, matrix products, body(): lax.dot_general(surface, panel, (((0,), (1,)), ((), ())), preferred_eleme...  26.4 us
    pallas_call x1, Pallas kernels, swap_after(): pl.pallas_call(functools.partial(swap_kernel, axis), out_shape=jax.ShapeD...  9.39 us
  transfers between devices with their start and end apart: 5, of which 2 were waited for; matrix products, arithmetic and copies ran while one was open for 18% of the time, Pallas kernels for 65%

profile of v2, /device:TPU:0, one launch (start us, length us, event | category | flops | bytes accessed | tf_op | source)
XLA Modules:
  0.0 349.3 jit_solution(17011075133090206615)
XLA Ops:
  0.0 0.5 collective-permute-start
  0.5 5.6 %slice.11 = bf16[768,3584]{1,0:T(8,128)(2,1)} slice(bf16[768,12288]{1,0:T(8,128)(2,1)} %refs_2_.11), slice={[0:768], [0:3584]} | slice | bytes 11010048 | tf_op jit(solution)/shard_map/slice | solution.py:215
  6.1 2.4 collective-permute-start.4
  8.5 26.4 %fusion.22 = f32[1024,768]{1,0:T(8,128)} fusion(bf16[12288,1024]{1,0:T(8,128)(2,1)} %param.7, bf16[768,12288]{1,0:T(8,128)(2,1)} %refs_2_.11), kind=kOutput, calls=%fused_computation.59 | convolution fusion | flops 19327352832 | bytes 47185920 | tf_op jit(solution)/shard_map/dot_general | solution.py:218
  34.9 51.5 %shard_map.64 = f32[4,32,768]{2,1,0:T(8,128)} custom-call(f32[4,8,32,768]{3,2,1,0:T(8,128)} %bitcast.89), custom_call_target="tpu_custom_call" | custom-call | tf_op jit(solution)/shard_map/pallas_call | solution.py:171
  86.5 1.8 bitcast_multiply_fusion.in_ref
  88.3 50.7 %shard_map.65 = f32[4,128,768]{2,1,0:T(8,128)} custom-call(f32[128,768]{1,0:T(8,128)} %bitcast_multiply_fusion.in_ref), custom_call_target="tpu_custom_call" | custom-call | tf_op jit(solution)/shard_map/pallas_call | solution.py:124
  139.0 3.0 copy.36
  142.0 3.1 copy.37
  145.3 0.6 gather_fusion.3
  145.8 1.2 gather_fusion
  147.1 0.8 scatter_custom_fusion
  148.0 2.0 gather_fusion.1
  150.0 0.1 select_bitcast_fusion
  150.1 0.2 copy.38
  150.3 2.8 broadcast_multiply_fusion.1
  153.1 15.2 %shard_map.66 = f32[4,128,768]{2,1,0:T(8,128)} custom-call(f32[128,768]{1,0:T(8,128)} %get-tuple-element.14.in_ref), custom_call_target="tpu_custom_call" | custom-call | tf_op jit(solution)/shard_map/pallas_call | solution.py:124
  168.3 0.7 fusion.14
  169.0 1.6 multiply_reduce_fusion
  170.7 0.9 copy.39
  171.6 1.2 copy.40
  172.8 0.9 fusion.27
  173.6 1.2 copy.41
  174.8 3.2 fusion.10.in_ref
  178.0 10.2 %shard_map.67 = bf16[4,128,768]{2,1,0:T(8,128)(2,1)} custom-call(bf16[128,768]{1,0:T(8,128)(2,1)} %fusion.10.in_ref), custom_call_target="tpu_custom_call" | custom-call | tf_op jit(solution)/shard_map/pallas_call | solution.py:124
  188.2 2.0 reshape.270
  190.2 0.1 constant_dynamic-slice_fusion.1
  190.6 0.6 gather_fusion.2
  191.2 0.6 gather_fusion.4
  191.8 0.1 copy_bitcast_fusion.1
  191.9 0.1 copy_bitcast_fusion
  192.0 0.7 pad_maximum_fusion.in_ref
  192.8 41.7 %shard_map.68 = bf16[8,32,4608]{2,1,0:T(8,128)(2,1)} custom-call(bf16[32,4608]{1,0:T(8,128)(2,1)} %pad_maximum_fusion.in_ref), custom_call_target="tpu_custom_call" | custom-call | tf_op jit(solution)/shard_map/pallas_call | solution.py:124
  234.5 1.7 copy-done.2
  236.1 6.8 %shard_map.71 = bf16[256,2560]{1,0:T(8,128)(2,1)} custom-call(bf16[256,4608]{1,0:T(8,128)(2,1)S(1)} %bitcast.72, bf16[256,4608]{1,0:T(8,128)(2,1)S(1)} %bitcast.73, bf16[768,12288]{1,0:T(8,128)(2,1)} %refs_2_.11, bf16[768,12288]{1,0:T(8,128)(2,1)} %collective-permute-done.refs_3_.refs_5_), custom_call_target="tpu_custom_call" | custom-call | flops 2013265920 | bytes 10485760 | tf_op jit(solution)/shard_map/pallas_call | solution.py:59
  243.0 1.5 collective-permute-start.3
  244.5 7.7 %shard_map.70 = bf16[256,3072]{1,0:T(8,128)(2,1)} custom-call(bf16[256,4608]{1,0:T(8,128)(2,1)S(1)} %bitcast.74, bf16[256,4608]{1,0:T(8,128)(2,1)S(1)} %bitcast.75, bf16[768,12288]{1,0:T(8,128)(2,1)} %refs_2_.11, bf16[768,12288]{1,0:T(8,128)(2,1)} %collective-permute-done.refs_3_.refs_5_), custom_call_target="tpu_custom_call" | custom-call | flops 2415919104 | bytes 12582912 | tf_op jit(solution)/shard_map/pallas_call | solution.py:59
  252.1 0.5 collective-permute-start.2
  252.7 7.6 %shard_map.69.token_ref = bf16[256,3072]{1,0:T(8,128)(2,1)} custom-call(bf16[256,4608]{1,0:T(8,128)(2,1)S(1)} %bitcast.76, bf16[256,4608]{1,0:T(8,128)(2,1)S(1)} %bitcast.77, bf16[768,12288]{1,0:T(8,128)(2,1)} %refs_2_.11, bf16[768,12288]{1,0:T(8,128)(2,1)} %collective-permute-done.refs_3_.refs_5_), custom_call_target="tpu_custom_call" | custom-call | flops 2415919104 | bytes 12582912 | tf_op jit(solution)/shard_map/pallas_call | solution.py:59
  260.3 1.5 collective-permute-start.1
  261.8 9.4 %shard_map.72.refs_7_ = bf16[768,3584]{1,0:T(8,128)(2,1)} custom-call(bf16[768,3584]{1,0:T(8,128)(2,1)} %collective-permute-done.4.in_ref.refs_6_, bf16[256,3072]{1,0:T(8,128)(2,1)} %shard_map.69.token_ref), custom_call_target="tpu_custom_call" | custom-call | tf_op jit(solution)/shard_map/pallas_call | solution.py:190
  271.2 2.6 copy-done.5
  273.8 11.9 %shard_map.73.refs_5_ = f32[256,12288]{1,0:T(8,128)} custom-call(bf16[256,4608]{1,0:T(8,128)(2,1)S(1)} %bitcast.78, bf16[256,4608]{1,0:T(8,128)(2,1)S(1)} %bitcast.79, bf16[256,4608]{1,0:T(8,128)(2,1)S(1)} %bitcast.80, bf16[256,4608]{1,0:T(8,128)(2,1)S(1)} %bitcast.81, bf16[768,12288]{1,0:T(8,128)(2,1)} %refs_2_.11, ...), custom_call_target="tpu_custom_call" | custom-call | flops 5637144576 | bytes 25690112 | tf_op jit(solution)/shard_map/pallas_call | solution.py:59
  285.7 7.7 %shard_map.74.refs_5_ = f32[256,12288]{1,0:T(8,128)} custom-call(bf16[256,4608]{1,0:T(8,128)(2,1)S(1)} %bitcast.82, bf16[256,4608]{1,0:T(8,128)(2,1)S(1)} %bitcast.83, bf16[768,12288]{1,0:T(8,128)(2,1)} %refs_2_.11, bf16[768,12288]{1,0:T(8,128)(2,1)} %collective-permute-done.refs_3_.refs_5_, ...), custom_call_target="tpu_custom_call", output_to_operand_aliasing={{}: (5, {})} | custom-call | flops 2013265920 | bytes 10485760 | tf_op jit(solution)/shard_map/pallas_call | solution.py:59
  293.4 15.3 %collective-permute-done.2.refs_4_ = bf16[256,3072]{1,0:T(8,128)(2,1)} collective-permute-done((bf16[256,3072]{1,0:T(8,128)(2,1)}, bf16[256,3072]{1,0:T(8,128)(2,1)}, u32[]{:S(2)}, u32[]{:S(2)}) %collective-permute-start.2) | collective-permute-done | bytes 1572896 | tf_op jit(solution)/shard_map/ppermute | solution.py:291
  308.7 8.3 %shard_map.75.refs_5_ = f32[256,12288]{1,0:T(8,128)} custom-call(bf16[256,4608]{1,0:T(8,128)(2,1)S(1)} %bitcast.84, bf16[256,4608]{1,0:T(8,128)(2,1)S(1)} %bitcast.85, bf16[768,12288]{1,0:T(8,128)(2,1)} %refs_2_.11, bf16[768,12288]{1,0:T(8,128)(2,1)} %collective-permute-done.refs_3_.refs_5_, ...), custom_call_target="tpu_custom_call", output_to_operand_aliasing={{}: (5, {})} | custom-call | flops 2415919104 | bytes 12582912 | tf_op jit(solution)/shard_map/pallas_call | solution.py:59
  317.0 23.9 %collective-permute-done.1.refs_4_ = bf16[256,3072]{1,0:T(8,128)(2,1)} collective-permute-done((bf16[256,3072]{1,0:T(8,128)(2,1)}, bf16[256,3072]{1,0:T(8,128)(2,1)}, u32[]{:S(2)}, u32[]{:S(2)}) %collective-permute-start.1) | collective-permute-done | bytes 1572896 | tf_op jit(solution)/shard_map/ppermute | solution.py:291
  340.8 8.5 %shard_map.76 = f32[256,12288]{1,0:T(8,128)} custom-call(bf16[256,4608]{1,0:T(8,128)(2,1)S(1)} %bitcast.86, bf16[256,4608]{1,0:T(8,128)(2,1)S(1)} %bitcast.87, bf16[768,12288]{1,0:T(8,128)(2,1)} %refs_2_.11, bf16[768,12288]{1,0:T(8,128)(2,1)} %collective-permute-done.refs_3_.refs_5_, ...), custom_call_target="tpu_custom_call", output_to_operand_aliasing={{}: (5, {})} | custom-call | flops 2415919104 | bytes 12582912 | tf_op jit(solution)/shard_map/pallas_call | solution.py:59
  (41 shorter events, 0.6 us)
Async XLA Ops:
  0.0 150.3 %copy-start = (f32[1,768,768]{2,1,0:T(8,128)S(1)}, f32[1,768,768]{2,1,0:T(8,128)}, u32[]{:S(2)}) copy-start(f32[1,768,768]{2,1,0:T(8,128)} %param.8) | copy-start | bytes 7077892
  0.0 234.5 %collective-permute-start = (bf16[768,12288]{1,0:T(8,128)(2,1)}, bf16[768,12288]{1,0:T(8,128)(2,1)}, u32[]{:S(2)}, u32[]{:S(2)}) collective-permute-start(bf16[768,12288]{1,0:T(8,128)(2,1)} %refs_2_.11), channel_id=1, source_target_pairs={{0,8},{8,0},{16,24},{24,16},{1,9},{9,1},{17,25},{25,17},{2,10},{10... | collective-permute-start | bytes 56623112 | tf_op jit(solution)/shard_map/ppermute | solution.py:216
  6.1 255.7 %collective-permute-start.4 = (bf16[768,3584]{1,0:T(8,128)(2,1)}, bf16[768,3584]{1,0:T(8,128)(2,1)}, u32[]{:S(2)}, u32[]{:S(2)}) collective-permute-start(bf16[768,3584]{1,0:T(8,128)(2,1)} %slice.11), channel_id=1, source_target_pairs={{0,16},{8,24},{16,0},{24,8},{1,17},{9,25},{17,1},{25,9},{2,18},{10... | collective-permute-start | bytes 16515080 | tf_op jit(solution)/shard_map/ppermute | solution.py:215
  34.9 51.5 %copy-start.8 = (s32[24]{0:T(128)S(1)}, s32[24]{0:T(128)}, u32[]{:S(2)}) copy-start(s32[24]{0:T(128)} %param.11) | copy-start | bytes 292
  142.0 3.8 %copy-start.6 = (s32[24]{0:T(128)S(1)}, s32[24]{0:T(128)}, u32[]{:S(2)}) copy-start(s32[24]{0:T(128)} %param.9) | copy-start | bytes 292
  178.0 12.4 %copy-start.7 = (s32[24]{0:T(128)S(1)}, s32[24]{0:T(128)}, u32[]{:S(2)}) copy-start(s32[24]{0:T(128)} %gather_fusion) | copy-start | bytes 292
  234.5 1.7 copy-start.2
  243.0 42.7 %collective-permute-start.3 = (bf16[256,2560]{1,0:T(8,128)(2,1)}, bf16[256,2560]{1,0:T(8,128)(2,1)}, u32[]{:S(2)}, u32[]{:S(2)}) collective-permute-start(bf16[256,2560]{1,0:T(8,128)(2,1)} %shard_map.71), channel_id=1, source_target_pairs={{0,16},{8,24},{16,0},{24,8},{1,17},{9,25},{17,1},{25,9},{2,18},{10... | collective-permute-start | bytes 3932168 | tf_op jit(solution)/shard_map/ppermute | solution.py:291
  252.1 56.5 %collective-permute-start.2 = (bf16[256,3072]{1,0:T(8,128)(2,1)}, bf16[256,3072]{1,0:T(8,128)(2,1)}, u32[]{:S(2)}, u32[]{:S(2)}) collective-permute-start(bf16[256,3072]{1,0:T(8,128)(2,1)} %shard_map.70), channel_id=1, source_target_pairs={{0,16},{8,24},{16,0},{24,8},{1,17},{9,25},{17,1},{25,9},{2,18},{10... | collective-permute-start | bytes 4718600 | tf_op jit(solution)/shard_map/ppermute | solution.py:291
  260.3 10.9 %copy-start.3 = (bf16[8,32,4608]{2,1,0:T(8,128)(2,1)S(1)}, bf16[8,32,4608]{2,1,0:T(8,128)(2,1)}, u32[]{:S(2)}) copy-start(bf16[8,32,4608]{2,1,0:T(8,128)(2,1)} %shard_map.68) | copy-start | bytes 7077892
  260.3 80.5 %collective-permute-start.1 = (bf16[256,3072]{1,0:T(8,128)(2,1)}, bf16[256,3072]{1,0:T(8,128)(2,1)}, u32[]{:S(2)}, u32[]{:S(2)}) collective-permute-start(bf16[256,3072]{1,0:T(8,128)(2,1)} %shard_map.69.token_ref), channel_id=1, source_target_pairs={{0,16},{8,24},{16,0},{24,8},{1,17},{9,25},{17,1},{25,9},{2,18},{10... | collective-permute-start | bytes 4718600 | tf_op jit(solution)/shard_map/ppermute | solution.py:291
  271.2 2.6 copy-start.5
  293.3 47.5 %copy-start.4 = (bf16[8,32,4608]{2,1,0:T(8,128)(2,1)S(1)}, bf16[8,32,4608]{2,1,0:T(8,128)(2,1)}, u32[]{:S(2)}) copy-start(bf16[8,32,4608]{2,1,0:T(8,128)(2,1)} %shard_map.68) | copy-start | bytes 7077892
  340.8 8.5 %copy-start.1 = (f32[1,768,768]{2,1,0:T(8,128)S(1)}, f32[1,768,768]{2,1,0:T(8,128)}, u32[]{:S(2)}) copy-start(f32[1,768,768]{2,1,0:T(8,128)} %param.8) | copy-start | bytes 7077892

commit v3 on v2

--- a/solution.py
+++ b/solution.py
@@ -8,14 +8,17 @@
 from jax.experimental.pallas import tpu as pltpu
 from jax.sharding import PartitionSpec as P
 
+
 MBLK = 128
 ITERS = 2
 DAMPING = 0.6
 COUPLING = 0.5
 TILE = 512
-GATHERED_SIXTEENTHS = 5
+EARLY_PART = 6
+LATE_PART = 12
+PARTS = 2
 MESH = pl.DeviceIdType.MESH
-PIECES = 3
+PIECE_EDGES = (0, 2, 8, 14, 17, 18)
 
 
 def live_pattern(live_rows):
@@ -23,7 +26,7 @@
     return (offsets[None, :] < live_rows[:, None]).astype(jnp.float32)
 
 
-def product_kernel(count, gain, with_extra, with_base, *refs):
+def product_kernel(count, gain, with_extra, *refs):
     factors, panels = refs[:count], refs[count : 2 * count]
     rest = refs[2 * count :]
     total = jnp.dot(factors[0][...], panels[0][...], preferred_element_type=jnp.float32)
@@ -35,7 +38,7 @@
     rest[-1][...] = total.astype(rest[-1].dtype)
 
 
-def product(loads, depth, first, panels, gain, columns, out_shape, out_start=0, extra=None, base=None):
+def product(loads, depth, first, panels, gain, columns, out_shape, out_start=0, extra=None, base=None, token=None):
     starts, width = columns
     count = len(panels)
     rows = loads.shape[0]
@@ -52,12 +55,15 @@
         in_specs.append(pl.BlockSpec((rows, TILE), lambda j: (0, j)))
         operands.append(extra)
     aliases = {}
+    if token is not None:
+        in_specs.append(pl.BlockSpec(memory_space=pl.ANY))
+        operands.append(token)
     if base is not None:
         in_specs.append(pl.BlockSpec(memory_space=pl.ANY))
         aliases = {len(operands): 0}
         operands.append(base)
     return pl.pallas_call(
-        functools.partial(product_kernel, count, gain, extra is not None, base is not None),
+        functools.partial(product_kernel, count, gain, extra is not None),
         grid=(width // TILE,),
         in_specs=in_specs,
         out_specs=pl.BlockSpec(
@@ -102,19 +108,39 @@
     partner = me + 1 - 2 * inner
     peers = [((place + k) % outer) * 2 + inner for k in range(1, outer)]
     greet(axis, [partner] + peers)
-    far = []
-    for k in range(1, outer):
-        far.append(
-            send(axis, peers[k - 1], in_ref, out_ref.at[me], far_send.at[k], far_recv.at[k])
-        )
-    near = [send(axis, partner, in_ref, out_ref.at[me], near_send.at[0], near_recv.at[0])]
+    width = in_ref.shape[-1] // PARTS
+    spans = [pl.ds(part * width, width) for part in range(PARTS)]
+    far, near = {}, []
+    for part, span in enumerate(spans):
+        near.append(
+            send(
+                axis,
+                partner,
+                in_ref.at[:, span],
+                out_ref.at[me, :, span],
+                near_send.at[0, part],
+                near_recv.at[0, part],
+            )
+        )
+        for k in range(1, outer):
+            far[part, k] = send(
+                axis,
+                peers[k - 1],
+                in_ref.at[:, span],
+                out_ref.at[me, :, span],
+                far_send.at[k, part],
+                far_recv.at[k, part],
+            )
     out_ref[me] = in_ref[...]
-    for k in range(1, outer):
-        source = ((place - k + outer) % outer) * 2 + inner
-        far[k - 1].wait_recv()
-        slot = out_ref.at[source]
-        near.append(send(axis, partner, slot, slot, near_send.at[k], near_recv.at[k]))
-    for copy in far:
+    for part, span in enumerate(spans):
+        for k in range(1, outer):
+            source = ((place - k + outer) % outer) * 2 + inner
+            far[part, k].wait_recv()
+            slot = out_ref.at[source, :, span]
+            near.append(
+                send(axis, partner, slot, slot, near_send.at[k, part], near_recv.at[k, part])
+            )
+    for copy in far.values():
         copy.wait_send()
     for copy in near:
         copy.wait()
@@ -126,9 +152,31 @@
         out_shape=jax.ShapeDtypeStruct((n,) + block.shape, block.dtype),
         in_specs=[pl.BlockSpec(memory_space=pltpu.VMEM)],
         out_specs=pl.BlockSpec(memory_space=pltpu.VMEM),
-        scratch_shapes=[pltpu.SemaphoreType.DMA((n // 2,))] * 4,
+        scratch_shapes=[pltpu.SemaphoreType.DMA((n // 2, PARTS))] * 4,
         compiler_params=pltpu.CompilerParams(collective_id=ident, has_side_effects=True),
     )(block)
+
+
+def pick_kernel(sources, block_ref, out_ref):
+    del sources
+    out_ref[...] = block_ref[0]
+
+
+def pick_blocks(every_block, sources):
+    rows, width = every_block.shape[1:]
+    per = width // MBLK
+    return pl.pallas_call(
+        pick_kernel,
+        grid_spec=pltpu.PrefetchScalarGridSpec(
+            num_scalar_prefetch=1,
+            grid=(sources.shape[0],),
+            in_specs=[
+                pl.BlockSpec((1, rows, MBLK), lambda j, at: (at[j] // per, 0, at[j] % per))
+            ],
+            out_specs=pl.BlockSpec((rows, MBLK), lambda j, at: (0, j)),
+        ),
+        out_shape=jax.ShapeDtypeStruct((rows, sources.shape[0] * MBLK), every_block.dtype),
+    )(sources, every_block)
 
 
 def reduce_kernel(axis, n, part, out_ref, near_in, held, far_in, near_send, near_recv, far_send, far_recv):
@@ -178,26 +226,29 @@
     )(partial)
 
 
-def swap_kernel(axis, in_ref, token_ref, out_ref, send_sem, recv_sem):
+def swap_kernel(axis, first_ref, second_ref, token_ref, first_out, second_out, send_sem, recv_sem):
     del token_ref
     me = lax.axis_index(axis)
     partner = me + 1 - 2 * (me % 2)
     greet(axis, [partner])
-    send(axis, partner, in_ref, out_ref, send_sem, recv_sem).wait()
-
-
-def swap_after(array, token, axis, ident):
+    first = send(axis, partner, first_ref, first_out, send_sem.at[0], recv_sem.at[0])
+    second = send(axis, partner, second_ref, second_out, send_sem.at[1], recv_sem.at[1])
+    first.wait()
+    second.wait()
+
+
+def swap_after(arrays, token, axis, ident):
     return pl.pallas_call(
         functools.partial(swap_kernel, axis),
-        out_shape=jax.ShapeDtypeStruct(array.shape, array.dtype),
-        in_specs=[pl.BlockSpec(memory_space=pl.ANY)] * 2,
-        out_specs=pl.BlockSpec(memory_space=pl.ANY),
-        scratch_shapes=[pltpu.SemaphoreType.DMA] * 2,
+        out_shape=[jax.ShapeDtypeStruct(array.shape, array.dtype) for array in arrays],
+        in_specs=[pl.BlockSpec(memory_space=pl.ANY)] * 3,
+        out_specs=[pl.BlockSpec(memory_space=pl.ANY)] * 2,
+        scratch_shapes=[pltpu.SemaphoreType.DMA((2,))] * 2,
         compiler_params=pltpu.CompilerParams(collective_id=ident, has_side_effects=True),
-    )(array, token)
-
-
-def body(panel, surface, flexibility, owner_map, adjacency, live_rows):
+    )(*arrays, token)
+
+
+def steps(panel, surface, flexibility, owner_map, adjacency, live_rows):
     order_rows, column_count = panel.shape
     row_total = lax.axis_size("row")
     col_total = lax.axis_size("col")
@@ -211,8 +262,10 @@
     swap = [(i, i ^ 1) for i in range(row_total)]
     across = [(i, i ^ 2) for i in range(row_total)]
 
-    gathered = max(TILE, column_count * GATHERED_SIXTEENTHS // 16 // TILE * TILE)
-    far = lax.ppermute(panel[:, :gathered], "row", across)
+    early = max(TILE, column_count // EARLY_PART // TILE * TILE)
+    late = max(TILE, column_count // LATE_PART // TILE * TILE)
+    gathered = early + late
+    far = lax.ppermute(panel[:, :early], "row", across)
     partner = lax.ppermute(panel, "row", swap)
 
     partial = lax.dot_general(
@@ -225,16 +278,13 @@
     own_pattern = lax.dynamic_slice_in_dim(pattern, own_row * block_count, block_count, 0)
     masked = traction * own_pattern.reshape(1, order_rows)
     every_block = gather(masked, "row", row_total, 1)
-    every_block = every_block.reshape(row_total, load_share, block_count, MBLK)
     inverse = (
         jnp.zeros((block_total,), jnp.int32)
         .at[owner_map]
         .set(jnp.arange(block_total, dtype=jnp.int32))
     )
     own_sources = lax.dynamic_slice_in_dim(inverse, own_row * block_count, block_count, 0)
-    every_block = every_block.transpose(0, 2, 1, 3).reshape(block_total, load_share, MBLK)
-    load_blocks = jnp.take(every_block, own_sources, axis=0)
-    load_blocks = load_blocks.transpose(1, 0, 2).reshape(load_share, order_rows)
+    load_blocks = pick_blocks(every_block, own_sources)
     hits = adjacency[0][:, None] == jnp.arange(row_total, dtype=jnp.int32)[None, :]
     neighbour_weights = jnp.sum(hits.astype(jnp.float32), axis=0)
     flex_local = flexibility[0]
@@ -255,6 +305,10 @@
         )
         traces = (1.0 - DAMPING) * traces + DAMPING * applied
     every_trace = gather(traces.astype(jnp.bfloat16), "row", row_total, 1 + ITERS)
+    late_panel, every_trace = lax.optimization_barrier(
+        (panel[:, early:gathered], every_trace)
+    )
+    far_late = lax.ppermute(late_panel, "row", across)
     every_trace = every_trace.reshape(row_total, row_total, small, block_count, MBLK)
     blocks = jnp.concatenate(
         [(own_row ^ k) * block_count + jnp.arange(block_count) for k in range(row_total)]
@@ -275,8 +329,9 @@
 
     gain = math.sqrt(column_count * col_total / (order_rows * row_total))
     width = column_count - gathered
-    edges = [width * k // PIECES // TILE * TILE for k in range(PIECES)] + [width]
-    arrivals = []
+    tiles = width // TILE
+    edges = sorted({tiles * edge // PIECE_EDGES[-1] * TILE for edge in PIECE_EDGES})
+    arrivals, piece = [], None
     for low, high in zip(edges[:-1], edges[1:]):
         start = gathered + low
         piece = product(
@@ -287,9 +342,10 @@
             gain,
             ([start, start], high - low),
             jax.ShapeDtypeStruct((group, high - low), jnp.bfloat16),
+            token=piece,
         )
         arrivals.append((start, high - low, lax.ppermute(piece, "row", across)))
-    far_partner = swap_after(far, piece, "row", 3 + ITERS)
+    far_partner, late_partner = swap_after([far, far_late], piece, "row", 3 + ITERS)
     full = jax.ShapeDtypeStruct((group, column_count), jnp.float32)
     response = product(
         all_loads,
@@ -297,8 +353,20 @@
         0,
         [panel, partner, far, far_partner],
         gain,
-        ([0] * row_total, gathered),
+        ([0] * row_total, early),
         full,
+    )
+    response = product(
+        all_loads,
+        order_rows,
+        0,
+        [panel, partner, far_late, late_partner],
+        gain,
+        ([early, early, 0, 0], late),
+        full,
+        early,
+        None,
+        response,
     )
     for start, size, arrived in arrivals:
         response = product(
@@ -319,4 +387,4 @@
 def solution(mesh):
     in_specs = (P("row", "col"), P("col", None), P("row", None, None), P(), P("row", None), P())
     out_specs = P("row", "col")
-    return jax.shard_map(body, mesh=mesh, in_specs=in_specs, out_specs=out_specs, check_vma=False)
+    return jax.shard_map(steps, mesh=mesh, in_specs=in_specs, out_specs=out_specs, check_vma=False)

time: 353 us -> 353 us (level)
  waiting for transfers between devices: 39.2 us -> 83.8 us
  Pallas kernels: 237 us -> 206 us
  local copies, waits for them, and re-layouts: 27.3 us -> 15.2 us
    ppermute x5 -> x8, waiting for transfers between devices: 39.2 us -> 83.8 us  [the longest x5 55.2 us: steps(): arrivals.append((start, high - low, lax.ppermute(piece, 'row', across)))]
    pallas_call x4, Pallas kernels: 118 us -> 74.7 us  [gather(): pl.pallas_call(functools.partial(gather_kernel, axis, n), out_shape=jax.S...]
    pallas_call x7 -> x12, Pallas kernels: 58.5 us -> 65 us  [product(): pl.pallas_call(functools.partial(product_kernel, count, gain, extra is no...]
    pallas_call x1 -> x2, Pallas kernels: 9.39 us -> 13 us  [the longest x1 8.29 us: swap_after(): pl.pallas_call(functools.partial(swap_kernel, axis), out_shape=[jax.Shape...]
    ppermute x5 -> x8, starting transfers between devices: 6.42 us -> 7.91 us  [the longest x5 5.33 us: steps(): arrivals.append((start, high - low, lax.ppermute(piece, 'row', across)))]
  transfers between devices with their start and end apart: 5 -> 8, of which waited for: 2 -> 2; matrix products, arithmetic and copies ran while one was open for 18% -> 14% of each run, Pallas kernels for 65% -> 58%
where the time goes in v3:
time: 353 us; the launch traced here: 351 us
  Pallas kernels  206 us (58%)
  waiting for transfers between devices  83.8 us (24%)
  matrix products  33.8 us (10%)
  local copies, waits for them, and re-layouts  15.2 us (4%)
  starting transfers between devices  7.91 us (2%)
  other arithmetic  4.81 us (1%)
    pallas_call x4, Pallas kernels, gather(): pl.pallas_call(functools.partial(gather_kernel, axis, n), out_shape=jax.S...  74.7 us
    pallas_call x12, Pallas kernels, product(): pl.pallas_call(functools.partial(product_kernel, count, gain, extra is no...  65 us
    ppermute x5, waiting for transfers between devices, steps(): arrivals.append((start, high - low, lax.ppermute(piece, 'row', across)))  55.2 us
    pallas_call x1, Pallas kernels, reduce_scatter(): pl.pallas_call(functools.partial(reduce_kernel, axis, n), out_shape=jax.S...  52.9 us
    ppermute x1, waiting for transfers between devices, steps(): far = lax.ppermute(panel[:, :early], 'row', across)  28.5 us
    dot_general x1, matrix products, steps(): lax.dot_general(surface, panel, (((0,), (1,)), ((), ())), preferred_eleme...  26.3 us
    pallas_call x1, Pallas kernels, swap_after(): pl.pallas_call(functools.partial(swap_kernel, axis), out_shape=[jax.Shape...  8.29 us
    dot_general x2, matrix products, steps(): lax.dot_general(coupled, flex_local, (((1,), (1,)), ((), ())), precision=...  7.47 us
  transfers between devices with their start and end apart: 8, of which 2 were waited for; matrix products, arithmetic and copies ran while one was open for 14% of the time, Pallas kernels for 58%

profile of v3, /device:TPU:0, one launch (start us, length us, event | category | flops | bytes accessed | tf_op | source)
XLA Modules:
  0.0 351.4 jit_solution(14202316113971670333)
XLA Ops:
  0.0 0.5 collective-permute-start
  0.5 2.9 slice.12
  3.4 26.3 %fusion.26 = f32[1024,768]{1,0:T(8,128)} fusion(bf16[12288,1024]{1,0:T(8,128)(2,1)} %param.7, bf16[768,12288]{1,0:T(8,128)(2,1)} %refs_2_.19), kind=kOutput, calls=%fused_computation.57 | convolution fusion | flops 19327352832 | bytes 47185920 | tf_op jit(solution)/shard_map/dot_general | solution.py:271
  29.8 52.9 %shard_map.64 = f32[4,32,768]{2,1,0:T(8,128)} custom-call(f32[4,8,32,768]{3,2,1,0:T(8,128)} %bitcast.89), custom_call_target="tpu_custom_call" | custom-call | tf_op jit(solution)/shard_map/pallas_call | solution.py:219
  82.7 0.6 scatter_custom_fusion
  83.3 0.7 dynamic_slice.13.sources
  84.1 1.8 bitcast_multiply_fusion.in_ref
  85.8 14.6 %shard_map.65.block_ref = f32[4,128,768]{2,1,0:T(8,128)} custom-call(f32[128,768]{1,0:T(8,128)} %bitcast_multiply_fusion.in_ref), custom_call_target="tpu_custom_call" | custom-call | tf_op jit(solution)/shard_map/pallas_call | solution.py:150
  100.5 4.7 %shard_map.66 = f32[128,768]{1,0:T(8,128)} custom-call(s32[6]{0:T(128)} %dynamic_slice.13.sources, f32[4,128,768]{2,1,0:T(8,128)} %shard_map.65.block_ref), custom_call_target="tpu_custom_call" | custom-call | tf_op jit(solution)/shard_map/pallas_call | solution.py:168
  105.2 4.3 %broadcast_multiply_fusion = (f32[128,768]{1,0:T(8,128)}, f32[128,768]{1,0:T(8,128)S(1)}) fusion(f32[128,768]{1,0:T(8,128)} %shard_map.66, f32[1,768,768]{2,1,0:T(8,128)S(1)} %copy-done), kind=kOutput, calls=%fused_computation.20 | convolution fusion | flops 906067968 | bytes 3538944 | tf_op jit(solution)/shard_map/dot_general | solution.py:299
  109.5 14.8 %shard_map.67 = f32[4,128,768]{2,1,0:T(8,128)} custom-call(f32[128,768]{1,0:T(8,128)} %get-tuple-element.20.in_ref), custom_call_target="tpu_custom_call" | custom-call | tf_op jit(solution)/shard_map/pallas_call | solution.py:150
  124.4 1.6 multiply_reduce_fusion
  126.0 3.2 fusion.10.in_ref
  129.2 10.1 %shard_map.68 = bf16[4,128,768]{2,1,0:T(8,128)(2,1)} custom-call(bf16[128,768]{1,0:T(8,128)(2,1)} %fusion.10.in_ref), custom_call_target="tpu_custom_call" | custom-call | tf_op jit(solution)/shard_map/pallas_call | solution.py:150
  139.3 1.3 collective-permute-start.6
  140.6 4.0 %slice.15 = bf16[768,2048]{1,0:T(8,128)(2,1)} slice(bf16[768,12288]{1,0:T(8,128)(2,1)} %refs_2_.19), slice={[0:768], [0:2048]} | slice | bytes 6291456 | tf_op jit(solution)/shard_map/slice | solution.py:268
  144.5 0.8 collective-permute-start.7
  145.4 0.7 gather_fusion
  146.1 0.6 gather_fusion.2
  146.9 0.9 reshape.249
  147.8 0.1 constant_dynamic-slice_fusion.1
  148.0 0.6 gather_fusion.1
  148.6 0.6 gather_fusion.3
  149.3 0.1 copy_bitcast_fusion
  149.4 0.8 pad_maximum_fusion.in_ref
  150.2 35.2 %shard_map.69 = bf16[8,32,4608]{2,1,0:T(8,128)(2,1)} custom-call(bf16[32,4608]{1,0:T(8,128)(2,1)} %pad_maximum_fusion.in_ref), custom_call_target="tpu_custom_call" | custom-call | tf_op jit(solution)/shard_map/pallas_call | solution.py:150
  185.4 1.7 copy-done.2
  187.1 3.3 shard_map.70.refs_4_
  190.4 7.6 %shard_map.71.refs_4_ = bf16[256,3072]{1,0:T(8,128)(2,1)} custom-call(bf16[256,4608]{1,0:T(8,128)(2,1)S(1)} %bitcast.63, bf16[256,4608]{1,0:T(8,128)(2,1)S(1)} %bitcast.64, bf16[768,12288]{1,0:T(8,128)(2,1)} %refs_2_.19, bf16[768,12288]{1,0:T(8,128)(2,1)} %collective-permute-done.refs_3_.refs_5_, bf16[256,1024]{1,0:T(8,128)(2,1)} %shard_map.70.refs_4_), custom_call_target="tpu_custom_call" | custom-call | flops 2415919104 | bytes 12582912 | tf_op jit(solution)/shard_map/pallas_call | solution.py:65
  198.0 1.3 collective-permute-start.4
  199.3 7.7 %shard_map.72.refs_4_ = bf16[256,3072]{1,0:T(8,128)(2,1)} custom-call(bf16[256,4608]{1,0:T(8,128)(2,1)S(1)} %bitcast.65, bf16[256,4608]{1,0:T(8,128)(2,1)S(1)} %bitcast.66, bf16[768,12288]{1,0:T(8,128)(2,1)} %refs_2_.19, bf16[768,12288]{1,0:T(8,128)(2,1)} %collective-permute-done.refs_3_.refs_5_, bf16[256,3072]{1,0:T(8,128)(2,1)} %shard_map.71.refs_4_), custom_call_target="tpu_custom_call" | custom-call | flops 2415919104 | bytes 12582912 | tf_op jit(solution)/shard_map/pallas_call | solution.py:65
  206.9 0.8 collective-permute-start.3
  207.7 1.3 collective-permute-start.5
  209.0 4.0 %shard_map.73.refs_4_ = bf16[256,1536]{1,0:T(8,128)(2,1)S(1)} custom-call(bf16[256,4608]{1,0:T(8,128)(2,1)S(1)} %bitcast.67, bf16[256,4608]{1,0:T(8,128)(2,1)S(1)} %bitcast.68, bf16[768,12288]{1,0:T(8,128)(2,1)} %refs_2_.19, bf16[768,12288]{1,0:T(8,128)(2,1)} %collective-permute-done.refs_3_.refs_5_, bf16[256,3072]{1,0:T(8,128)(2,1)} %shard_map.72.refs_4_), custom_call_target="tpu_custom_call" | custom-call | flops 1207959552 | bytes 6291456 | tf_op jit(solution)/shard_map/pallas_call | solution.py:65
  212.9 2.0 shard_map.74.token_ref
  215.0 0.8 collective-permute-start.2
  215.8 28.5 %collective-permute-done.7.first_ref.refs_6_ = bf16[768,2048]{1,0:T(8,128)(2,1)} collective-permute-done((bf16[768,2048]{1,0:T(8,128)(2,1)}, bf16[768,2048]{1,0:T(8,128)(2,1)}, u32[]{:S(2)}, u32[]{:S(2)}) %collective-permute-start.7) | collective-permute-done | bytes 3145760 | tf_op jit(solution)/shard_map/ppermute | solution.py:268
  244.3 1.2 collective-permute-start.1
  245.6 8.3 %shard_map.75 = (bf16[768,2048]{1,0:T(8,128)(2,1)}, bf16[768,1024]{1,0:T(8,128)(2,1)}) custom-call(bf16[768,2048]{1,0:T(8,128)(2,1)} %collective-permute-done.7.first_ref.refs_6_, bf16[768,1024]{1,0:T(8,128)(2,1)} %collective-permute-done.6.second_ref.refs_6_, bf16[256,512]{1,0:T(8,128)(2,1)} %copy-done.7), custom_call_target="tpu_custom_call" | custom-call | tf_op jit(solution)/shard_map/pallas_call | solution.py:241
  253.9 1.9 copy-done.5
  255.8 7.6 %shard_map.76.refs_8_ = f32[256,12288]{1,0:T(8,128)} custom-call(bf16[256,4608]{1,0:T(8,128)(2,1)S(1)} %bitcast.74, bf16[256,4608]{1,0:T(8,128)(2,1)S(1)} %bitcast.72, bf16[256,4608]{1,0:T(8,128)(2,1)S(1)} %bitcast.73, bf16[256,4608]{1,0:T(8,128)(2,1)S(1)} %bitcast.71, bf16[768,12288]{1,0:T(8,128)(2,1)} %refs_2_.19, ...), custom_call_target="tpu_custom_call" | custom-call | flops 3221225472 | bytes 14680064 | tf_op jit(solution)/shard_map/pallas_call | solution.py:65
  263.3 4.4 %shard_map.77.refs_5_ = f32[256,12288]{1,0:T(8,128)} custom-call(bf16[256,4608]{1,0:T(8,128)(2,1)S(1)} %bitcast.75, bf16[256,4608]{1,0:T(8,128)(2,1)S(1)} %bitcast.76, bf16[256,4608]{1,0:T(8,128)(2,1)S(1)} %bitcast.77, bf16[256,4608]{1,0:T(8,128)(2,1)S(1)} %bitcast.78, bf16[768,12288]{1,0:T(8,128)(2,1)} %refs_2_.19, ...), custom_call_target="tpu_custom_call", output_to_operand_aliasing={{}: (8, {})} | custom-call | flops 1610612736 | bytes 7340032 | tf_op jit(solution)/shard_map/pallas_call | solution.py:65
  267.8 55.2 %collective-permute-done.5.refs_4_ = bf16[256,1024]{1,0:T(8,128)(2,1)} collective-permute-done((bf16[256,1024]{1,0:T(8,128)(2,1)}, bf16[256,1024]{1,0:T(8,128)(2,1)}, u32[]{:S(2)}, u32[]{:S(2)}) %collective-permute-start.5) | collective-permute-done | bytes 524320 | tf_op jit(solution)/shard_map/ppermute | solution.py:347
  323.0 3.4 shard_map.78.refs_5_
  326.4 8.3 %shard_map.79.refs_5_ = f32[256,12288]{1,0:T(8,128)} custom-call(bf16[256,4608]{1,0:T(8,128)(2,1)S(1)} %bitcast.81, bf16[256,4608]{1,0:T(8,128)(2,1)S(1)} %bitcast.82, bf16[768,12288]{1,0:T(8,128)(2,1)} %refs_2_.19, bf16[768,12288]{1,0:T(8,128)(2,1)} %collective-permute-done.refs_3_.refs_5_, ...), custom_call_target="tpu_custom_call", output_to_operand_aliasing={{}: (5, {})} | custom-call | flops 2415919104 | bytes 12582912 | tf_op jit(solution)/shard_map/pallas_call | solution.py:65
  334.7 8.3 %shard_map.80.refs_5_ = f32[256,12288]{1,0:T(8,128)} custom-call(bf16[256,4608]{1,0:T(8,128)(2,1)S(1)} %bitcast.83, bf16[256,4608]{1,0:T(8,128)(2,1)S(1)} %bitcast.84, bf16[768,12288]{1,0:T(8,128)(2,1)} %refs_2_.19, bf16[768,12288]{1,0:T(8,128)(2,1)} %collective-permute-done.refs_3_.refs_5_, ...), custom_call_target="tpu_custom_call", output_to_operand_aliasing={{}: (5, {})} | custom-call | flops 2415919104 | bytes 12582912 | tf_op jit(solution)/shard_map/pallas_call | solution.py:65
  343.1 5.4 %shard_map.81.refs_5_ = f32[256,12288]{1,0:T(8,128)} custom-call(bf16[256,4608]{1,0:T(8,128)(2,1)S(1)} %bitcast.85, bf16[256,4608]{1,0:T(8,128)(2,1)S(1)} %bitcast.86, bf16[768,12288]{1,0:T(8,128)(2,1)} %refs_2_.19, bf16[768,12288]{1,0:T(8,128)(2,1)} %collective-permute-done.refs_3_.refs_5_, ...), custom_call_target="tpu_custom_call", output_to_operand_aliasing={{}: (5, {})} | custom-call | flops 1207959552 | bytes 6291456 | tf_op jit(solution)/shard_map/pallas_call | solution.py:65
  348.5 3.0 shard_map.82
  (51 shorter events, 0.7 us)
Async XLA Ops:
  0.0 105.2 %copy-start = (f32[1,768,768]{2,1,0:T(8,128)S(1)}, f32[1,768,768]{2,1,0:T(8,128)}, u32[]{:S(2)}) copy-start(f32[1,768,768]{2,1,0:T(8,128)} %param.8) | copy-start | bytes 7077892
  0.0 185.4 %collective-permute-start = (bf16[768,12288]{1,0:T(8,128)(2,1)}, bf16[768,12288]{1,0:T(8,128)(2,1)}, u32[]{:S(2)}, u32[]{:S(2)}) collective-permute-start(bf16[768,12288]{1,0:T(8,128)(2,1)} %refs_2_.19), channel_id=1, source_target_pairs={{0,8},{8,0},{16,24},{24,16},{1,9},{9,1},{17,25},{25,17},{2,10},{10... | collective-permute-start | bytes 56623112 | tf_op jit(solution)/shard_map/ppermute | solution.py:269
  29.7 52.9 %copy-start.8 = (s32[24]{0:T(128)S(1)}, s32[24]{0:T(128)}, u32[]{:S(2)}) copy-start(s32[24]{0:T(128)} %param.9) | copy-start | bytes 292
  29.7 54.2 %copy-start.11 = (s32[24]{0:T(128)S(1)}, s32[24]{0:T(128)}, u32[]{:S(2)}) copy-start(s32[24]{0:T(128)} %param.11) | copy-start | bytes 292
  105.2 19.1 %copy-start.12 = (s32[1,2]{1,0:T(1,128)S(1)}, s32[1,2]{1,0:T(1,128)}, u32[]{:S(2)}) copy-start(s32[1,2]{1,0:T(1,128)} %param.10) | copy-start | bytes 28
  105.2 20.8 %copy-start.9 = (f32[128,768]{1,0:T(8,128)S(1)}, f32[128,768]{1,0:T(8,128)}, u32[]{:S(2)}) copy-start(f32[128,768]{1,0:T(8,128)} %shard_map.66) | copy-start | bytes 1179652
  139.3 7.6 %copy-start.10 = (bf16[4,128,768]{2,1,0:T(8,128)(2,1)S(1)}, bf16[4,128,768]{2,1,0:T(8,128)(2,1)}, u32[]{:S(2)}) copy-start(bf16[4,128,768]{2,1,0:T(8,128)(2,1)} %shard_map.68) | copy-start | bytes 2359300
  139.3 75.7 %collective-permute-start.6 = (bf16[768,1024]{1,0:T(8,128)(2,1)}, bf16[768,1024]{1,0:T(8,128)(2,1)}, u32[]{:S(2)}, u32[]{:S(2)}) collective-permute-start(bf16[768,1024]{1,0:T(8,128)(2,1)} %slice.12), channel_id=1, source_target_pairs={{0,16},{8,24},{16,0},{24,8},{1,17},{9,25},{17,1},{25,9},{2,18},{10... | collective-permute-start | bytes 4718600 | tf_op jit(solution)/shard_map/ppermute | solution.py:311
  144.5 99.8 %collective-permute-start.7 = (bf16[768,2048]{1,0:T(8,128)(2,1)}, bf16[768,2048]{1,0:T(8,128)(2,1)}, u32[]{:S(2)}, u32[]{:S(2)}) collective-permute-start(bf16[768,2048]{1,0:T(8,128)(2,1)} %slice.15), channel_id=1, source_target_pairs={{0,16},{8,24},{16,0},{24,8},{1,17},{9,25},{17,1},{25,9},{2,18},{10... | collective-permute-start | bytes 9437192 | tf_op jit(solution)/shard_map/ppermute | solution.py:268
  185.4 1.7 copy-start.2
  198.0 128.4 %collective-permute-start.4 = (bf16[256,3072]{1,0:T(8,128)(2,1)}, bf16[256,3072]{1,0:T(8,128)(2,1)}, u32[]{:S(2)}, u32[]{:S(2)}) collective-permute-start(bf16[256,3072]{1,0:T(8,128)(2,1)} %shard_map.71.refs_4_), channel_id=1, source_target_pairs={{0,16},{8,24},{16,0},{24,8},{1,17},{9,25},{17,1},{25,9},{2,18},{10... | collective-permute-start | bytes 4718600 | tf_op jit(solution)/shard_map/ppermute | solution.py:347
  206.9 127.8 %collective-permute-start.3 = (bf16[256,3072]{1,0:T(8,128)(2,1)}, bf16[256,3072]{1,0:T(8,128)(2,1)}, u32[]{:S(2)}, u32[]{:S(2)}) collective-permute-start(bf16[256,3072]{1,0:T(8,128)(2,1)} %shard_map.72.refs_4_), channel_id=1, source_target_pairs={{0,16},{8,24},{16,0},{24,8},{1,17},{9,25},{17,1},{25,9},{2,18},{10... | collective-permute-start | bytes 4718600 | tf_op jit(solution)/shard_map/ppermute | solution.py:347
  207.7 115.3 %collective-permute-start.5 = (bf16[256,1024]{1,0:T(8,128)(2,1)}, bf16[256,1024]{1,0:T(8,128)(2,1)}, u32[]{:S(2)}, u32[]{:S(2)}) collective-permute-start(bf16[256,1024]{1,0:T(8,128)(2,1)} %shard_map.70.refs_4_), channel_id=1, source_target_pairs={{0,16},{8,24},{16,0},{24,8},{1,17},{9,25},{17,1},{25,9},{2,18},{10... | collective-permute-start | bytes 1572872 | tf_op jit(solution)/shard_map/ppermute | solution.py:347
  214.9 30.6 %copy-start.7 = (bf16[256,512]{1,0:T(8,128)(2,1)}, bf16[256,512]{1,0:T(8,128)(2,1)S(1)}, u32[]{:S(2)}) copy-start(bf16[256,512]{1,0:T(8,128)(2,1)S(1)} %shard_map.74.token_ref) | copy-start | bytes 786436
  215.0 38.9 %copy-start.3 = (bf16[8,32,4608]{2,1,0:T(8,128)(2,1)S(1)}, bf16[8,32,4608]{2,1,0:T(8,128)(2,1)}, u32[]{:S(2)}) copy-start(bf16[8,32,4608]{2,1,0:T(8,128)(2,1)} %shard_map.69) | copy-start | bytes 7077892
  215.0 128.1 %collective-permute-start.2 = (bf16[256,1536]{1,0:T(8,128)(2,1)S(1)}, bf16[256,1536]{1,0:T(8,128)(2,1)}, u32[]{:S(2)}, u32[]{:S(2)}) collective-permute-start(bf16[256,1536]{1,0:T(8,128)(2,1)S(1)} %shard_map.73.refs_4_), channel_id=1, source_target_pairs={{0,16},{8,24},{16,0},{24,8},{1,17},{9,25},{17,1},{25,9},{2,18},{10... | collective-permute-start | bytes 2359304 | tf_op jit(solution)/shard_map/ppermute | solution.py:347
  244.3 104.1 %collective-permute-start.1 = (bf16[256,512]{1,0:T(8,128)(2,1)S(1)}, bf16[256,512]{1,0:T(8,128)(2,1)}, u32[]{:S(2)}, u32[]{:S(2)}) collective-permute-start(bf16[256,512]{1,0:T(8,128)(2,1)S(1)} %shard_map.74.token_ref), channel_id=1, source_target_pairs={{0,16},{8,24},{16,0},{24,8},{1,17},{9,25},{17,1},{25,9},{2,18},{10... | collective-permute-start | bytes 786440 | tf_op jit(solution)/shard_map/ppermute | solution.py:347
  253.9 1.9 copy-start.5
  255.8 7.6 %copy-start.6 = (bf16[768,1024]{1,0:T(8,128)(2,1)S(1)}, bf16[768,1024]{1,0:T(8,128)(2,1)}, u32[]{:S(2)}) copy-start(bf16[768,1024]{1,0:T(8,128)(2,1)} %get-tuple-element.11.refs_7_) | copy-start | bytes 4718596
  343.1 5.4 %copy-start.4 = (bf16[8,32,4608]{2,1,0:T(8,128)(2,1)S(1)}, bf16[8,32,4608]{2,1,0:T(8,128)(2,1)}, u32[]{:S(2)}) copy-start(bf16[8,32,4608]{2,1,0:T(8,128)(2,1)} %shard_map.69) | copy-start | bytes 7077892
  348.5 3.0 copy-start.1

commit v4 on v3

--- a/solution.py
+++ b/solution.py
@@ -14,9 +14,11 @@
 DAMPING = 0.6
 COUPLING = 0.5
 TILE = 512
-EARLY_PART = 6
-LATE_PART = 12
-PARTS = 2
+EARLY_PART = 5
+LATE_PART = 2
+WHOLE_PART = 24
+PARTS = 3
+HALVES = 2
 MESH = pl.DeviceIdType.MESH
 PIECE_EDGES = (0, 2, 8, 14, 17, 18)
 
@@ -185,31 +187,42 @@
     partner = me + 1 - 2 * inner
     peers = [((place + k) % outer) * 2 + inner for k in range(outer)]
     greet(axis, [partner] + peers[1:])
-    order = list(range(1, outer)) + [0]
+    depth = part.shape[0] // HALVES
+    order = [(k, h) for k in list(range(1, outer)) + [0] for h in range(HALVES)]
+    spans = [pl.ds(h * depth, depth) for h in range(HALVES)]
     near = {}
-    for k in order:
-        near[k] = send(
+    for k, h in order:
+        near[k, h] = send(
             axis,
             partner,
-            part.at[:, peers[k] + 1 - 2 * inner],
-            near_in.at[k],
-            near_send.at[k],
-            near_recv.at[k],
+            part.at[spans[h], peers[k] + 1 - 2 * inner],
+            near_in.at[k, spans[h]],
+            near_send.at[k, h],
+            near_recv.at[k, h],
         )
     far = {}
-    for k in order[:-1]:
-        near[k].wait_recv()
-        held[k] = part[:, peers[k]] + near_in[k]
-        far[k] = send(axis, peers[k], held.at[k], far_in.at[k], far_send.at[k], far_recv.at[k])
-    near[0].wait_recv()
-    out_ref[...] = part[:, me] + near_in[0]
-    for k in order[:-1]:
-        far[k].wait_recv()
-        out_ref[...] += far_in[k]
-    for k in order[:-1]:
-        far[k].wait_send()
-    for k in order:
-        near[k].wait_send()
+    for k, h in order:
+        near[k, h].wait_recv()
+        span = spans[h]
+        if k == 0:
+            out_ref[span] = part[span, me] + near_in[0, span]
+            continue
+        held[k, span] = part[span, peers[k]] + near_in[k, span]
+        far[k, h] = send(
+            axis,
+            peers[k],
+            held.at[k, span],
+            far_in.at[k, span],
+            far_send.at[k, h],
+            far_recv.at[k, h],
+        )
+    for k, h in far:
+        far[k, h].wait_recv()
+        out_ref[spans[h]] += far_in[k, spans[h]]
+    for copy in far.values():
+        copy.wait_send()
+    for copy in near.values():
+        copy.wait_send()
 
 
 def reduce_scatter(partial, axis, n, ident):
@@ -221,7 +234,7 @@
         out_shape=jax.ShapeDtypeStruct(block, jnp.float32),
         in_specs=[pl.BlockSpec(memory_space=pltpu.VMEM)],
         out_specs=pl.BlockSpec(memory_space=pltpu.VMEM),
-        scratch_shapes=[slots] * 3 + [pltpu.SemaphoreType.DMA((n // 2,))] * 4,
+        scratch_shapes=[slots] * 3 + [pltpu.SemaphoreType.DMA((n // 2, HALVES))] * 4,
         compiler_params=pltpu.CompilerParams(collective_id=ident, has_side_effects=True),
     )(partial)
 
@@ -262,8 +275,8 @@
     swap = [(i, i ^ 1) for i in range(row_total)]
     across = [(i, i ^ 2) for i in range(row_total)]
 
-    early = max(TILE, column_count // EARLY_PART // TILE * TILE)
-    late = max(TILE, column_count // LATE_PART // TILE * TILE)
+    early = max(TILE, column_count * EARLY_PART // WHOLE_PART // TILE * TILE)
+    late = max(TILE, column_count * LATE_PART // WHOLE_PART // TILE * TILE)
     gathered = early + late
     far = lax.ppermute(panel[:, :early], "row", across)
     partner = lax.ppermute(panel, "row", swap)

time: 353 us -> 359 us (1.017)
  waiting for transfers between devices: 83.8 us -> 92 us
    ppermute x1, waiting for transfers between devices: 28.5 us -> 45.3 us  [steps(): far = lax.ppermute(panel[:, :early], 'row', across)]
    ppermute x5, waiting for transfers between devices: 55.2 us -> 46.7 us  [steps(): arrivals.append((start, high - low, lax.ppermute(piece, 'row', across)))]
    pallas_call x1, Pallas kernels: 52.9 us -> 48.8 us  [reduce_scatter(): pl.pallas_call(functools.partial(reduce_kernel, axis, n), out_shape=jax.S...]
  transfers between devices with their start and end apart: 8 -> 8, of which waited for: 2 -> 2; matrix products, arithmetic and copies ran while one was open for 14% -> 14% of each run, Pallas kernels for 58% -> 56%
where the time goes in v4:
time: 359 us; the launch traced here: 358 us
  Pallas kernels  203 us (57%)
  waiting for transfers between devices  92 us (26%)
  matrix products  33.8 us (9%)
  local copies, waits for them, and re-layouts  15.8 us (4%)
  starting transfers between devices  7.85 us (2%)
  other arithmetic  4.79 us (1%)
    pallas_call x4, Pallas kernels, gather(): pl.pallas_call(functools.partial(gather_kernel, axis, n), out_shape=jax.S...  75.2 us
    pallas_call x12, Pallas kernels, product(): pl.pallas_call(functools.partial(product_kernel, count, gain, extra is no...  65.3 us
    pallas_call x1, Pallas kernels, reduce_scatter(): pl.pallas_call(functools.partial(reduce_kernel, axis, n), out_shape=jax.S...  48.8 us
    ppermute x5, waiting for transfers between devices, steps(): arrivals.append((start, high - low, lax.ppermute(piece, 'row', across)))  46.7 us
    ppermute x1, waiting for transfers between devices, steps(): far = lax.ppermute(panel[:, :early], 'row', across)  45.3 us
    dot_general x1, matrix products, steps(): lax.dot_general(surface, panel, (((0,), (1,)), ((), ())), preferred_eleme...  26.3 us
    pallas_call x1, Pallas kernels, swap_after(): pl.pallas_call(functools.partial(swap_kernel, axis), out_shape=[jax.Shape...  9.41 us
    dot_general x2, matrix products, steps(): lax.dot_general(coupled, flex_local, (((1,), (1,)), ((), ())), precision=...  7.47 us
  transfers between devices with their start and end apart: 8, of which 2 were waited for; matrix products, arithmetic and copies ran while one was open for 14% of the time, Pallas kernels for 56%

profile of v4, /device:TPU:0, one launch (start us, length us, event | category | flops | bytes accessed | tf_op | source)
XLA Modules:
  0.0 357.9 jit_solution(8343250060379815887)
XLA Ops:
  0.0 0.5 collective-permute-start
  0.5 2.9 slice.12
  3.4 26.3 %fusion.26 = f32[1024,768]{1,0:T(8,128)} fusion(bf16[12288,1024]{1,0:T(8,128)(2,1)} %param.7, bf16[768,12288]{1,0:T(8,128)(2,1)} %refs_2_.19), kind=kOutput, calls=%fused_computation.57 | convolution fusion | flops 19327352832 | bytes 47185920 | tf_op jit(solution)/shard_map/dot_general | solution.py:284
  29.7 48.8 %shard_map.64 = f32[4,32,768]{2,1,0:T(8,128)} custom-call(f32[4,8,32,768]{3,2,1,0:T(8,128)} %bitcast.89), custom_call_target="tpu_custom_call" | custom-call | tf_op jit(solution)/shard_map/pallas_call | solution.py:232
  78.6 0.6 scatter_custom_fusion
  79.2 0.6 dynamic_slice.13.sources
  79.9 1.8 bitcast_multiply_fusion.in_ref
  81.7 14.6 %shard_map.65.block_ref = f32[4,128,768]{2,1,0:T(8,128)} custom-call(f32[128,768]{1,0:T(8,128)} %bitcast_multiply_fusion.in_ref), custom_call_target="tpu_custom_call" | custom-call | tf_op jit(solution)/shard_map/pallas_call | solution.py:152
  96.3 4.7 %shard_map.66 = f32[128,768]{1,0:T(8,128)} custom-call(s32[6]{0:T(128)} %dynamic_slice.13.sources, f32[4,128,768]{2,1,0:T(8,128)} %shard_map.65.block_ref), custom_call_target="tpu_custom_call" | custom-call | tf_op jit(solution)/shard_map/pallas_call | solution.py:170
  101.1 4.3 %broadcast_multiply_fusion = (f32[128,768]{1,0:T(8,128)}, f32[128,768]{1,0:T(8,128)S(1)}) fusion(f32[128,768]{1,0:T(8,128)} %shard_map.66, f32[1,768,768]{2,1,0:T(8,128)S(1)} %copy-done), kind=kOutput, calls=%fused_computation.20 | convolution fusion | flops 906067968 | bytes 3538944 | tf_op jit(solution)/shard_map/dot_general | solution.py:312
  105.4 14.7 %shard_map.67 = f32[4,128,768]{2,1,0:T(8,128)} custom-call(f32[128,768]{1,0:T(8,128)} %get-tuple-element.20.in_ref), custom_call_target="tpu_custom_call" | custom-call | tf_op jit(solution)/shard_map/pallas_call | solution.py:152
  120.2 1.6 multiply_reduce_fusion
  121.9 3.2 fusion.10.in_ref
  125.0 10.2 %shard_map.68 = bf16[4,128,768]{2,1,0:T(8,128)(2,1)} custom-call(bf16[128,768]{1,0:T(8,128)(2,1)} %fusion.10.in_ref), custom_call_target="tpu_custom_call" | custom-call | tf_op jit(solution)/shard_map/pallas_call | solution.py:152
  135.2 1.3 collective-permute-start.6
  136.5 4.3 %slice.15 = bf16[768,2560]{1,0:T(8,128)(2,1)} slice(bf16[768,12288]{1,0:T(8,128)(2,1)} %refs_2_.19), slice={[0:768], [0:2560]} | slice | bytes 7864320 | tf_op jit(solution)/shard_map/slice | solution.py:281
  140.8 0.8 collective-permute-start.7
  141.7 0.7 gather_fusion
  142.4 0.6 gather_fusion.2
  143.1 0.9 reshape.249
  144.0 0.1 constant_dynamic-slice_fusion.1
  144.2 0.6 gather_fusion.1
  144.9 0.6 gather_fusion.3
  145.5 0.1 copy_bitcast_fusion
  145.7 0.7 pad_maximum_fusion.in_ref
  146.4 35.7 %shard_map.69 = bf16[8,32,4608]{2,1,0:T(8,128)(2,1)} custom-call(bf16[32,4608]{1,0:T(8,128)(2,1)} %pad_maximum_fusion.in_ref), custom_call_target="tpu_custom_call" | custom-call | tf_op jit(solution)/shard_map/pallas_call | solution.py:152
  182.1 1.7 copy-done.2
  183.8 2.0 shard_map.70.refs_4_
  185.8 7.7 %shard_map.71.refs_4_ = bf16[256,3072]{1,0:T(8,128)(2,1)} custom-call(bf16[256,4608]{1,0:T(8,128)(2,1)S(1)} %bitcast.63, bf16[256,4608]{1,0:T(8,128)(2,1)S(1)} %bitcast.64, bf16[768,12288]{1,0:T(8,128)(2,1)} %refs_2_.19, bf16[768,12288]{1,0:T(8,128)(2,1)} %collective-permute-done.refs_3_.refs_5_, bf16[256,512]{1,0:T(8,128)(2,1)S(1)} %shard_map.70.refs_4_), custom_call_target="tpu_custom_call" | custom-call | flops 2415919104 | bytes 12582912 | tf_op jit(solution)/shard_map/pallas_call | solution.py:67
  193.4 1.3 collective-permute-start.4
  194.7 7.7 %shard_map.72.refs_4_ = bf16[256,3072]{1,0:T(8,128)(2,1)} custom-call(bf16[256,4608]{1,0:T(8,128)(2,1)S(1)} %bitcast.65, bf16[256,4608]{1,0:T(8,128)(2,1)S(1)} %bitcast.66, bf16[768,12288]{1,0:T(8,128)(2,1)} %refs_2_.19, bf16[768,12288]{1,0:T(8,128)(2,1)} %collective-permute-done.refs_3_.refs_5_, bf16[256,3072]{1,0:T(8,128)(2,1)} %shard_map.71.refs_4_), custom_call_target="tpu_custom_call" | custom-call | flops 2415919104 | bytes 12582912 | tf_op jit(solution)/shard_map/pallas_call | solution.py:67
  202.3 0.8 collective-permute-start.3
  203.1 1.3 collective-permute-start.5
  204.4 4.0 %shard_map.73.refs_4_ = bf16[256,1536]{1,0:T(8,128)(2,1)S(1)} custom-call(bf16[256,4608]{1,0:T(8,128)(2,1)S(1)} %bitcast.67, bf16[256,4608]{1,0:T(8,128)(2,1)S(1)} %bitcast.68, bf16[768,12288]{1,0:T(8,128)(2,1)} %refs_2_.19, bf16[768,12288]{1,0:T(8,128)(2,1)} %collective-permute-done.refs_3_.refs_5_, bf16[256,3072]{1,0:T(8,128)(2,1)} %shard_map.72.refs_4_), custom_call_target="tpu_custom_call" | custom-call | flops 1207959552 | bytes 6291456 | tf_op jit(solution)/shard_map/pallas_call | solution.py:67
  208.3 2.7 shard_map.74.token_ref
  211.0 0.8 collective-permute-start.2
  211.8 45.3 %collective-permute-done.7.first_ref.refs_6_ = bf16[768,2560]{1,0:T(8,128)(2,1)} collective-permute-done((bf16[768,2560]{1,0:T(8,128)(2,1)}, bf16[768,2560]{1,0:T(8,128)(2,1)}, u32[]{:S(2)}, u32[]{:S(2)}) %collective-permute-start.7) | collective-permute-done | bytes 3932192 | tf_op jit(solution)/shard_map/ppermute | solution.py:281
  257.1 1.2 collective-permute-start.1
  258.3 9.4 %shard_map.75 = (bf16[768,2560]{1,0:T(8,128)(2,1)}, bf16[768,1024]{1,0:T(8,128)(2,1)}) custom-call(bf16[768,2560]{1,0:T(8,128)(2,1)} %collective-permute-done.7.first_ref.refs_6_, bf16[768,1024]{1,0:T(8,128)(2,1)} %collective-permute-done.6.second_ref.refs_6_, bf16[256,512]{1,0:T(8,128)(2,1)} %shard_map.74.token_ref), custom_call_target="tpu_custom_call" | custom-call | tf_op jit(solution)/shard_map/pallas_call | solution.py:254
  267.8 2.1 copy-done.5
  269.9 9.2 %shard_map.76.refs_8_ = f32[256,12288]{1,0:T(8,128)} custom-call(bf16[256,4608]{1,0:T(8,128)(2,1)S(1)} %bitcast.74, bf16[256,4608]{1,0:T(8,128)(2,1)S(1)} %bitcast.72, bf16[256,4608]{1,0:T(8,128)(2,1)S(1)} %bitcast.73, bf16[256,4608]{1,0:T(8,128)(2,1)S(1)} %bitcast.71, bf16[768,12288]{1,0:T(8,128)(2,1)} %refs_2_.19, ...), custom_call_target="tpu_custom_call" | custom-call | flops 4026531840 | bytes 18350080 | tf_op jit(solution)/shard_map/pallas_call | solution.py:67
  279.0 4.4 %shard_map.77.refs_5_ = f32[256,12288]{1,0:T(8,128)} custom-call(bf16[256,4608]{1,0:T(8,128)(2,1)S(1)} %bitcast.75, bf16[256,4608]{1,0:T(8,128)(2,1)S(1)} %bitcast.76, bf16[256,4608]{1,0:T(8,128)(2,1)S(1)} %bitcast.77, bf16[256,4608]{1,0:T(8,128)(2,1)S(1)} %bitcast.78, bf16[768,12288]{1,0:T(8,128)(2,1)} %refs_2_.19, ...), custom_call_target="tpu_custom_call", output_to_operand_aliasing={{}: (8, {})} | custom-call | flops 1610612736 | bytes 7340032 | tf_op jit(solution)/shard_map/pallas_call | solution.py:67
  283.5 46.7 %collective-permute-done.5.refs_4_ = bf16[256,512]{1,0:T(8,128)(2,1)} collective-permute-done((bf16[256,512]{1,0:T(8,128)(2,1)S(1)}, bf16[256,512]{1,0:T(8,128)(2,1)}, u32[]{:S(2)}, u32[]{:S(2)}) %collective-permute-start.5) | collective-permute-done | bytes 262176 | tf_op jit(solution)/shard_map/ppermute | solution.py:360
  330.1 2.8 shard_map.78.refs_5_
  333.0 8.3 %shard_map.79.refs_5_ = f32[256,12288]{1,0:T(8,128)} custom-call(bf16[256,4608]{1,0:T(8,128)(2,1)S(1)} %bitcast.81, bf16[256,4608]{1,0:T(8,128)(2,1)S(1)} %bitcast.82, bf16[768,12288]{1,0:T(8,128)(2,1)} %refs_2_.19, bf16[768,12288]{1,0:T(8,128)(2,1)} %collective-permute-done.refs_3_.refs_5_, ...), custom_call_target="tpu_custom_call", output_to_operand_aliasing={{}: (5, {})} | custom-call | flops 2415919104 | bytes 12582912 | tf_op jit(solution)/shard_map/pallas_call | solution.py:67
  341.3 8.3 %shard_map.80.refs_5_ = f32[256,12288]{1,0:T(8,128)} custom-call(bf16[256,4608]{1,0:T(8,128)(2,1)S(1)} %bitcast.83, bf16[256,4608]{1,0:T(8,128)(2,1)S(1)} %bitcast.84, bf16[768,12288]{1,0:T(8,128)(2,1)} %refs_2_.19, bf16[768,12288]{1,0:T(8,128)(2,1)} %collective-permute-done.refs_3_.refs_5_, ...), custom_call_target="tpu_custom_call", output_to_operand_aliasing={{}: (5, {})} | custom-call | flops 2415919104 | bytes 12582912 | tf_op jit(solution)/shard_map/pallas_call | solution.py:67
  349.6 5.4 %shard_map.81.refs_5_ = f32[256,12288]{1,0:T(8,128)} custom-call(bf16[256,4608]{1,0:T(8,128)(2,1)S(1)} %bitcast.85, bf16[256,4608]{1,0:T(8,128)(2,1)S(1)} %bitcast.86, bf16[768,12288]{1,0:T(8,128)(2,1)} %refs_2_.19, bf16[768,12288]{1,0:T(8,128)(2,1)} %collective-permute-done.refs_3_.refs_5_, ...), custom_call_target="tpu_custom_call", output_to_operand_aliasing={{}: (5, {})} | custom-call | flops 1207959552 | bytes 6291456 | tf_op jit(solution)/shard_map/pallas_call | solution.py:67
  355.0 3.0 shard_map.82
  (49 shorter events, 0.7 us)
Async XLA Ops:
  0.0 101.1 %copy-start = (f32[1,768,768]{2,1,0:T(8,128)S(1)}, f32[1,768,768]{2,1,0:T(8,128)}, u32[]{:S(2)}) copy-start(f32[1,768,768]{2,1,0:T(8,128)} %param.8) | copy-start | bytes 7077892
  0.0 182.1 %collective-permute-start = (bf16[768,12288]{1,0:T(8,128)(2,1)}, bf16[768,12288]{1,0:T(8,128)(2,1)}, u32[]{:S(2)}, u32[]{:S(2)}) collective-permute-start(bf16[768,12288]{1,0:T(8,128)(2,1)} %refs_2_.19), channel_id=1, source_target_pairs={{0,8},{8,0},{16,24},{24,16},{1,9},{9,1},{17,25},{25,17},{2,10},{10... | collective-permute-start | bytes 56623112 | tf_op jit(solution)/shard_map/ppermute | solution.py:282
  29.7 48.8 %copy-start.7 = (s32[24]{0:T(128)S(1)}, s32[24]{0:T(128)}, u32[]{:S(2)}) copy-start(s32[24]{0:T(128)} %param.9) | copy-start | bytes 292
  29.7 50.1 %copy-start.10 = (s32[24]{0:T(128)S(1)}, s32[24]{0:T(128)}, u32[]{:S(2)}) copy-start(s32[24]{0:T(128)} %param.11) | copy-start | bytes 292
  101.1 19.1 %copy-start.11 = (s32[1,2]{1,0:T(1,128)S(1)}, s32[1,2]{1,0:T(1,128)}, u32[]{:S(2)}) copy-start(s32[1,2]{1,0:T(1,128)} %param.10) | copy-start | bytes 28
  101.1 20.8 %copy-start.8 = (f32[128,768]{1,0:T(8,128)S(1)}, f32[128,768]{1,0:T(8,128)}, u32[]{:S(2)}) copy-start(f32[128,768]{1,0:T(8,128)} %shard_map.66) | copy-start | bytes 1179652
  135.2 8.0 %copy-start.9 = (bf16[4,128,768]{2,1,0:T(8,128)(2,1)S(1)}, bf16[4,128,768]{2,1,0:T(8,128)(2,1)}, u32[]{:S(2)}) copy-start(bf16[4,128,768]{2,1,0:T(8,128)(2,1)} %shard_map.68) | copy-start | bytes 2359300
  135.2 75.8 %collective-permute-start.6 = (bf16[768,1024]{1,0:T(8,128)(2,1)}, bf16[768,1024]{1,0:T(8,128)(2,1)}, u32[]{:S(2)}, u32[]{:S(2)}) collective-permute-start(bf16[768,1024]{1,0:T(8,128)(2,1)} %slice.12), channel_id=1, source_target_pairs={{0,16},{8,24},{16,0},{24,8},{1,17},{9,25},{17,1},{25,9},{2,18},{10... | collective-permute-start | bytes 4718600 | tf_op jit(solution)/shard_map/ppermute | solution.py:324
  140.8 116.4 %collective-permute-start.7 = (bf16[768,2560]{1,0:T(8,128)(2,1)}, bf16[768,2560]{1,0:T(8,128)(2,1)}, u32[]{:S(2)}, u32[]{:S(2)}) collective-permute-start(bf16[768,2560]{1,0:T(8,128)(2,1)} %slice.15), channel_id=1, source_target_pairs={{0,16},{8,24},{16,0},{24,8},{1,17},{9,25},{17,1},{25,9},{2,18},{10... | collective-permute-start | bytes 11796488 | tf_op jit(solution)/shard_map/ppermute | solution.py:281
  182.1 1.7 copy-start.2
  193.4 139.5 %collective-permute-start.4 = (bf16[256,3072]{1,0:T(8,128)(2,1)}, bf16[256,3072]{1,0:T(8,128)(2,1)}, u32[]{:S(2)}, u32[]{:S(2)}) collective-permute-start(bf16[256,3072]{1,0:T(8,128)(2,1)} %shard_map.71.refs_4_), channel_id=1, source_target_pairs={{0,16},{8,24},{16,0},{24,8},{1,17},{9,25},{17,1},{25,9},{2,18},{10... | collective-permute-start | bytes 4718600 | tf_op jit(solution)/shard_map/ppermute | solution.py:360
  202.3 138.9 %collective-permute-start.3 = (bf16[256,3072]{1,0:T(8,128)(2,1)}, bf16[256,3072]{1,0:T(8,128)(2,1)}, u32[]{:S(2)}, u32[]{:S(2)}) collective-permute-start(bf16[256,3072]{1,0:T(8,128)(2,1)} %shard_map.72.refs_4_), channel_id=1, source_target_pairs={{0,16},{8,24},{16,0},{24,8},{1,17},{9,25},{17,1},{25,9},{2,18},{10... | collective-permute-start | bytes 4718600 | tf_op jit(solution)/shard_map/ppermute | solution.py:360
  203.1 127.0 %collective-permute-start.5 = (bf16[256,512]{1,0:T(8,128)(2,1)S(1)}, bf16[256,512]{1,0:T(8,128)(2,1)}, u32[]{:S(2)}, u32[]{:S(2)}) collective-permute-start(bf16[256,512]{1,0:T(8,128)(2,1)S(1)} %shard_map.70.refs_4_), channel_id=1, source_target_pairs={{0,16},{8,24},{16,0},{24,8},{1,17},{9,25},{17,1},{25,9},{2,18},{10... | collective-permute-start | bytes 786440 | tf_op jit(solution)/shard_map/ppermute | solution.py:360
  211.0 56.7 %copy-start.3 = (bf16[8,32,4608]{2,1,0:T(8,128)(2,1)S(1)}, bf16[8,32,4608]{2,1,0:T(8,128)(2,1)}, u32[]{:S(2)}) copy-start(bf16[8,32,4608]{2,1,0:T(8,128)(2,1)} %shard_map.69) | copy-start | bytes 7077892
  211.0 138.5 %collective-permute-start.2 = (bf16[256,1536]{1,0:T(8,128)(2,1)S(1)}, bf16[256,1536]{1,0:T(8,128)(2,1)}, u32[]{:S(2)}, u32[]{:S(2)}) collective-permute-start(bf16[256,1536]{1,0:T(8,128)(2,1)S(1)} %shard_map.73.refs_4_), channel_id=1, source_target_pairs={{0,16},{8,24},{16,0},{24,8},{1,17},{9,25},{17,1},{25,9},{2,18},{10... | collective-permute-start | bytes 2359304 | tf_op jit(solution)/shard_map/ppermute | solution.py:360
  257.1 97.9 %collective-permute-start.1 = (bf16[256,512]{1,0:T(8,128)(2,1)}, bf16[256,512]{1,0:T(8,128)(2,1)}, u32[]{:S(2)}, u32[]{:S(2)}) collective-permute-start(bf16[256,512]{1,0:T(8,128)(2,1)} %shard_map.74.token_ref), channel_id=1, source_target_pairs={{0,16},{8,24},{16,0},{24,8},{1,17},{9,25},{17,1},{25,9},{2,18},{10... | collective-permute-start | bytes 786440 | tf_op jit(solution)/shard_map/ppermute | solution.py:360
  267.7 2.1 copy-start.5
  269.9 9.2 %copy-start.6 = (bf16[768,1024]{1,0:T(8,128)(2,1)S(1)}, bf16[768,1024]{1,0:T(8,128)(2,1)}, u32[]{:S(2)}) copy-start(bf16[768,1024]{1,0:T(8,128)(2,1)} %get-tuple-element.11.refs_7_) | copy-start | bytes 4718596
  349.6 5.4 %copy-start.4 = (bf16[8,32,4608]{2,1,0:T(8,128)(2,1)S(1)}, bf16[8,32,4608]{2,1,0:T(8,128)(2,1)}, u32[]{:S(2)}) copy-start(bf16[8,32,4608]{2,1,0:T(8,128)(2,1)} %shard_map.69) | copy-start | bytes 7077892
  355.0 3.0 copy-start.1
